TPU v7x, 32 devices: a whole 2x2x4 slice. The times are simulated.
32 devices in a mesh: sec: 4 (over y, core), grp: 8 (over z, x).
Axes of the slice: x: 2, y: 2, z: 4, core: 2. Of those that a mesh axis runs over, the one named last changes fastest.
Arguments:
- solution_in: float32 [2, 32, 4, 6144], P(None, 'grp', None, 'sec'), may hold values from -6 to 6
- residual_in: float32 [2, 32, 4, 6144], P(None, 'grp', None, 'sec'), may hold values from -6 to 6
- direction_in: float32 [2, 32, 4, 6144], P(None, 'grp', None, 'sec'), may hold values from -6 to 6
- legendre: bfloat16 [32, 2, 128, 6144], P('grp', None, None, 'sec'), may hold values from -0.0034179688 to 0.0034179688
- inverse_prior: float32 [2, 6144], P(None, 'sec'), may hold values from 0.3 to 10
- noise_qq: float32 [128, 8192], P('grp', 'sec'), may hold values from 0.5 to 4
- noise_qu: float32 [128, 8192], P('grp', 'sec'), may hold values from -0.3 to 0.3
- noise_uu: float32 [128, 8192], P('grp', 'sec'), may hold values from 0.5 to 4
- pixel_mask: int32 [128, 8192], P('grp', 'sec'), may hold values 0 or 1
- cycle_phase: float32 [128], replicated, as said below
- m_values: int32 [32], replicated, may hold values from 0 to 6143, as said below
Outputs:
- solution: float32 [2, 32, 4, 6144], P(None, 'grp', None, 'sec')
- residual: float32 [2, 32, 4, 6144], P(None, 'grp', None, 'sec')
- direction: float32 [2, 32, 4, 6144], P(None, 'grp', None, 'sec')
Inputs may be any that keep to these rules, and one draw needn't show every extreme that they name: `m_values`: the slots' m values are distinct, and exactly one slot has m = 0. `cycle_phase`: each phase lies between 0 and 2 pi / 8192.
All inputs are finite; a program needn't handle non-finite values. No bound on the sum of `pixel_mask` on one device may be relied on, other than what follows from the above.
Results may differ from a plain program's by a relative error of at most 0.025.
Values sent between devices are 32-bit elements; how exact they have to be, the bound alone decides.
No kernel may reach another device: no remote copies, remote signals or barrier semaphores. Data moves between devices by JAX's collectives and lax.ppermute only.
A program may use at most 64 MiB of HBM per device.

v0:
```python
import math

import jax
import jax.numpy as jnp
from jax import lax
from jax.sharding import PartitionSpec as P

ITERS = 4


full_turn = 2.0 * math.pi


def combine_modes(prod):
    plus = prod[:, :, 0]
    minus = prod[:, :, 1]
    return jnp.stack(
        [
            -plus[:, :, 0] + minus[:, :, 3],
            -plus[:, :, 1] - minus[:, :, 2],
            -plus[:, :, 2] - minus[:, :, 1],
            -plus[:, :, 3] + minus[:, :, 0],
        ],
        axis=2,
    )


def adjoint_terms(field):
    half = field.astype(jnp.bfloat16)
    minus_part = jnp.stack([half[:, :, 3], -half[:, :, 2], -half[:, :, 1], half[:, :, 0]], axis=2)
    return jnp.stack([-half, minus_part], axis=2)


def legendre_forward(coeffs, legendre):
    half = coeffs.astype(jnp.bfloat16)
    prod = jnp.einsum("msrl,bmcl->bmscr", legendre, half, preferred_element_type=jnp.float32)
    return combine_modes(prod)


def legendre_adjoint(field, legendre):
    both = adjoint_terms(field)
    return jnp.einsum("msrl,bmscr->bmcl", legendre, both, preferred_element_type=jnp.float32)


def phi_table(m_values, start, count, total):
    index = start + jnp.arange(count, dtype=jnp.int32)
    folded = m_values[:, None] * index[None, :] % total
    angle = folded.astype(jnp.float32) * (full_turn / total)
    weight = jnp.where(m_values == 0, 1.0, 2.0).astype(jnp.float32)[:, None]
    return jnp.concatenate([weight * jnp.cos(angle), -weight * jnp.sin(angle)], axis=0)


def pixel_segment(field, cosines, sine_table, table, noise_qq, noise_qu, noise_uu, mask_f):
    count = field.shape[0]
    modes = field.shape[1]
    cycles = field.shape[3]
    parts = field.reshape(count, modes, 2, 2, cycles)
    real = parts[:, :, :, 0]
    imag = parts[:, :, :, 1]
    cosm = cosines[None, :, None, :]
    sinm = sine_table[None, :, None, :]
    rot_re = real * cosm - imag * sinm
    rot_im = real * sinm + imag * cosm
    rows = (
        jnp.stack([rot_re, rot_im], axis=1)
        .transpose(0, 3, 4, 1, 2)
        .reshape(count * 2 * cycles, 2 * modes)
    )
    pixels = jnp.dot(
        rows, table, precision=lax.Precision.HIGHEST, preferred_element_type=jnp.float32
    )
    pixels = pixels.reshape(count, 2, cycles, -1)
    qpart = pixels[:, 0]
    upart = pixels[:, 1]
    wq = mask_f * (noise_qq * qpart + noise_qu * upart)
    wu = mask_f * (noise_qu * qpart + noise_uu * upart)
    weighted = jnp.stack([wq, wu], axis=1).reshape(count * 2 * cycles, -1)
    back = jnp.dot(
        weighted, table.T, precision=lax.Precision.HIGHEST, preferred_element_type=jnp.float32
    )
    back = back.reshape(count, 2, cycles, 2, modes)
    out = jnp.stack([back[:, :, :, 0], back[:, :, :, 1]], axis=2)
    return out.transpose(0, 4, 1, 2, 3).reshape(count, modes, 4, cycles)


def rotate_back(field, cosines, sine_table):
    count = field.shape[0]
    modes = field.shape[1]
    cycles = field.shape[3]
    parts = field.reshape(count, modes, 2, 2, cycles)
    real = parts[:, :, :, 0]
    imag = parts[:, :, :, 1]
    cosm = cosines[None, :, None, :]
    sinm = sine_table[None, :, None, :]
    turned_real = real * cosm + imag * sinm
    turned_imag = imag * cosm - real * sinm
    return jnp.stack([turned_real, turned_imag], axis=3).reshape(count, modes, 4, cycles)


def totals(values):
    return jnp.sum(values, axis=(1, 2, 3))


def per_device(
    solution_in,
    residual_in,
    direction_in,
    legendre,
    inverse_prior,
    noise_qq,
    noise_qu,
    noise_uu,
    pixel_mask,
    cycle_phase,
    m_values,
):
    phi_local = noise_qq.shape[1]
    cycles_here = noise_qq.shape[0]
    modes_here = solution_in.shape[1]
    sections = lax.axis_size("sec")
    group_index = lax.axis_index("grp")
    local_phase = lax.dynamic_slice_in_dim(cycle_phase, group_index * cycles_here, cycles_here, 0)
    angle = m_values.astype(jnp.float32)[:, None] * local_phase[None, :]
    cosines = jnp.cos(angle)
    sine_table = jnp.sin(angle)
    local_m = lax.dynamic_slice_in_dim(m_values, group_index * modes_here, modes_here, 0)
    slot_angle = local_m.astype(jnp.float32)[:, None] * cycle_phase[None, :]
    slot_cos = jnp.cos(slot_angle)
    slot_sin = jnp.sin(slot_angle)
    mask_f = pixel_mask.astype(jnp.float32)
    prior = jnp.repeat(inverse_prior, 2, axis=0)[None, None]
    table = phi_table(m_values, lax.axis_index("sec") * phi_local, phi_local, phi_local * sections)
    solution, residual, direction = (solution_in, residual_in, direction_in)
    for step in range(ITERS):
        apply_field = legendre_forward(direction, legendre)
        field = lax.all_to_all(apply_field, "grp", split_axis=3, concat_axis=1, tiled=True)
        field = lax.psum(field, "sec")
        partial_field = pixel_segment(
            field, cosines, sine_table, table, noise_qq, noise_qu, noise_uu, mask_f
        )
        folded = lax.all_to_all(partial_field, "grp", split_axis=1, concat_axis=3, tiled=True)
        folded = lax.psum(folded, "sec")
        mode_field = rotate_back(folded, slot_cos, slot_sin)
        image = prior * direction + legendre_adjoint(mode_field, legendre)
        norm_now, curve, cross, square = lax.psum(
            (
                totals(residual * residual),
                totals(direction * image),
                totals(residual * image),
                totals(image * image),
            ),
            ("sec", "grp"),
        )
        step_size = norm_now / curve
        alpha = step_size[:, None, None, None]
        solution = solution + alpha * direction
        residual = residual - alpha * image
        norm_next = norm_now - 2.0 * step_size * cross + step_size * step_size * square
        direction = residual + (norm_next / norm_now)[:, None, None, None] * direction
    return (solution, residual, direction)


def solution(mesh):
    return jax.shard_map(
        per_device,
        mesh=mesh,
        in_specs=(
            P(None, "grp", None, "sec"),
            P(None, "grp", None, "sec"),
            P(None, "grp", None, "sec"),
            P("grp", None, None, "sec"),
            P(None, "sec"),
            P("grp", "sec"),
            P("grp", "sec"),
            P("grp", "sec"),
            P("grp", "sec"),
            P(),
            P(),
        ),
        out_specs=(
            P(None, "grp", None, "sec"),
            P(None, "grp", None, "sec"),
            P(None, "grp", None, "sec"),
        ),
        check_vma=False,
    )
```

profile of v0, /device:TPU:0, one launch (start us, length us, event | category | flops | bytes accessed | tf_op | source)
XLA Modules:
  0.0 451.1 jit_solution(6203677750327580794)
XLA Ops:
  0.7 1.9 copy-done
  2.5 1.9 fusion.40
  5.5 2.4 reshape.484
  7.9 7.3 %all-to-all-start = ((f32[8,1,512]{2,1,0:T(1,128)}), f32[8,1,512]{2,1,0:T(1,128)S(1)}, u32[]{:S(2)}, u32[]{:S(2)}) async-start(f32[8,1,512]{2,1,0:T(1,128)} %reshape.484), calls=%async_computation | async-start | bytes 32768 | tf_op jit(solution)/shard_map/all_to_all | solution.py:136
  15.5 1.1 cosine_multiply_fusion
  18.3 1.6 convert_element_type.80
  19.8 1.9 all-to-all-done
  22.9 1.6 reshape.485
  24.6 2.2 copy.135
  26.8 12.4 %psum.169 = f32[2,32,2,2,16]{4,1,3,2,0:T(8,128)} all-reduce(f32[2,32,2,2,16]{4,1,3,2,0:T(8,128)} %bitcast.348), channel_id=1, replica_groups=mesh['sec'=4,'grp'=8] {'sec'}, use_global_device_ids=true, to_apply=%region_2.3 | all-reduce | flops 4096 | bytes 32768 | tf_op jit(solution)/shard_map/psum | solution.py:137
  42.5 1.5 fusion.70
  44.1 1.2 add_multiply_fusion.7
  45.3 2.5 fusion.52
  48.6 1.6 reshape.486
  50.2 4.5 all-to-all-start.1
  54.7 1.1 multiply_reduce_fusion.15
  55.8 5.5 %all-to-all-done.1 = f32[8,1,512]{2,1,0:T(1,128)S(1)} async-done(((f32[8,1,512]{2,1,0:T(1,128)}), f32[8,1,512]{2,1,0:T(1,128)S(1)}, u32[]{:S(2)}, u32[]{:S(2)}) %all-to-all-start.1) | async-done | bytes 16416 | tf_op jit(solution)/shard_map/all_to_all | solution.py:141
  65.4 10.1 %psum.170 = f32[2,4,2,2,128]{4,3,2,1,0:T(2,128)S(1)} all-reduce(f32[2,4,2,2,128]{4,3,2,1,0:T(2,128)S(1)} %reshape.451), channel_id=1, replica_groups=mesh['sec'=4,'grp'=8] {'sec'}, use_global_device_ids=true, to_apply=%region_3.4 | all-reduce | flops 4096 | bytes 32768 | tf_op jit(solution)/shard_map/psum | solution.py:142
  75.6 2.2 multiply_reduce_fusion.12
  77.9 38.3 %all-reduce.3 = (f32[2]{0:T(128)S(1)}, f32[2]{0:T(128)S(1)}, f32[2]{0:T(128)S(1)}, f32[2]{0:T(128)S(1)}) all-reduce(f32[2]{0:T(128)S(1)} %multiply_reduce_fusion.15, f32[2]{0:T(128)S(1)} %get-tuple-element.29, f32[2]{0:T(128)S(1)} %get-tuple-element.28, f32[2]{0:T(128)S(1)} %get-tuple-element.27), channel_id=1, replica_groups=mesh['sec'=4,'grp'=8] {'sec','grp'}, use_global_device_ids=true, to_apply=%region_1.2 | all-reduce | flops 8 | bytes 64 | tf_op jit(solution)/shard_map/psum | solution.py:145
  116.2 1.9 multiply_add_fusion.3
  119.9 1.0 copy.152
  120.9 1.8 reshape.488
  122.7 10.9 %all_to_all.144 = f32[8,1,512]{2,1,0:T(1,128)S(1)} all-to-all(f32[8,1,512]{2,1,0:T(1,128)S(1)} %reshape.488), channel_id=1, replica_groups=mesh['sec'=4,'grp'=8] {'grp'}, dimensions={0} | all-to-all | bytes 32768 | tf_op jit(solution)/shard_map/all_to_all | solution.py:136
  134.3 1.6 reshape.489
  135.9 2.2 copy.153
  138.1 1.6 copy.154
  139.7 12.6 %psum.175 = f32[2,32,2,2,16]{4,1,2,0,3:T(8,128)} all-reduce(f32[2,32,2,2,16]{4,1,2,0,3:T(8,128)} %copy.154), channel_id=1, replica_groups=mesh['sec'=4,'grp'=8] {'sec'}, use_global_device_ids=true, to_apply=%region_12.13 | all-reduce | flops 4096 | bytes 32768 | tf_op jit(solution)/shard_map/psum | solution.py:137
  155.6 1.5 fusion.68
  157.1 1.2 add_multiply_fusion.5
  158.4 2.5 fusion.55
  162.7 8.9 %all_to_all.145 = f32[8,1,512]{2,1,0:T(1,128)S(1)} all-to-all(f32[8,1,512]{2,1,0:T(1,128)S(1)} %reshape.490), channel_id=1, replica_groups=mesh['sec'=4,'grp'=8] {'grp'}, dimensions={0} | all-to-all | bytes 32768 | tf_op jit(solution)/shard_map/all_to_all | solution.py:141
  175.7 10.1 %psum.176 = f32[2,4,2,2,128]{4,3,2,1,0:T(2,128)S(1)} all-reduce(f32[2,4,2,2,128]{4,3,2,1,0:T(2,128)S(1)} %reshape.454), channel_id=1, replica_groups=mesh['sec'=4,'grp'=8] {'sec'}, use_global_device_ids=true, to_apply=%region_13.14 | all-reduce | flops 4096 | bytes 32768 | tf_op jit(solution)/shard_map/psum | solution.py:142
  186.0 2.2 multiply_reduce_fusion.8
  188.2 38.7 %all-reduce.2 = (f32[2]{0:T(128)S(1)}, f32[2]{0:T(128)S(1)}, f32[2]{0:T(128)S(1)}, f32[2]{0:T(128)S(1)}) all-reduce(f32[2]{0:T(128)S(1)} %get-tuple-element.26, f32[2]{0:T(128)S(1)} %get-tuple-element.25, f32[2]{0:T(128)S(1)} %get-tuple-element.24, f32[2]{0:T(128)S(1)} %get-tuple-element.23), channel_id=1, replica_groups=mesh['sec'=4,'grp'=8] {'sec','grp'}, use_global_device_ids=true, to_apply=%region_7.8 | all-reduce | flops 8 | bytes 64 | tf_op jit(solution)/shard_map/psum | solution.py:145
  227.0 1.9 multiply_add_fusion.2
  231.7 1.8 reshape.492
  233.4 10.9 %all_to_all.146 = f32[8,1,512]{2,1,0:T(1,128)S(1)} all-to-all(f32[8,1,512]{2,1,0:T(1,128)S(1)} %reshape.492), channel_id=1, replica_groups=mesh['sec'=4,'grp'=8] {'grp'}, dimensions={0} | all-to-all | bytes 32768 | tf_op jit(solution)/shard_map/all_to_all | solution.py:136
  245.0 1.6 reshape.493
  246.7 2.2 copy.165
  248.9 1.6 copy.166
  250.4 12.4 %psum.181 = f32[2,32,2,2,16]{4,1,2,0,3:T(8,128)} all-reduce(f32[2,32,2,2,16]{4,1,2,0,3:T(8,128)} %copy.166), channel_id=1, replica_groups=mesh['sec'=4,'grp'=8] {'sec'}, use_global_device_ids=true, to_apply=%region_22.23 | all-reduce | flops 4096 | bytes 32768 | tf_op jit(solution)/shard_map/psum | solution.py:137
  266.1 1.5 fusion.66
  267.7 1.2 add_multiply_fusion.3
  268.9 2.5 fusion.58
  273.2 8.9 %all_to_all.147 = f32[8,1,512]{2,1,0:T(1,128)S(1)} all-to-all(f32[8,1,512]{2,1,0:T(1,128)S(1)} %reshape.494), channel_id=1, replica_groups=mesh['sec'=4,'grp'=8] {'grp'}, dimensions={0} | all-to-all | bytes 32768 | tf_op jit(solution)/shard_map/all_to_all | solution.py:141
  286.2 10.1 %psum.182 = f32[2,4,2,2,128]{4,3,2,1,0:T(2,128)S(1)} all-reduce(f32[2,4,2,2,128]{4,3,2,1,0:T(2,128)S(1)} %reshape.457), channel_id=1, replica_groups=mesh['sec'=4,'grp'=8] {'sec'}, use_global_device_ids=true, to_apply=%region_23.24 | all-reduce | flops 4096 | bytes 32768 | tf_op jit(solution)/shard_map/psum | solution.py:142
  296.5 2.2 multiply_reduce_fusion.4
  298.7 38.7 %all-reduce.1 = (f32[2]{0:T(128)S(1)}, f32[2]{0:T(128)S(1)}, f32[2]{0:T(128)S(1)}, f32[2]{0:T(128)S(1)}) all-reduce(f32[2]{0:T(128)S(1)} %get-tuple-element.22, f32[2]{0:T(128)S(1)} %get-tuple-element.21, f32[2]{0:T(128)S(1)} %get-tuple-element.20, f32[2]{0:T(128)S(1)} %get-tuple-element.19), channel_id=1, replica_groups=mesh['sec'=4,'grp'=8] {'sec','grp'}, use_global_device_ids=true, to_apply=%region_17.18 | all-reduce | flops 8 | bytes 64 | tf_op jit(solution)/shard_map/psum | solution.py:145
  337.5 1.9 multiply_add_fusion.1
  342.2 1.8 reshape.496
  344.0 10.9 %all_to_all.148 = f32[8,1,512]{2,1,0:T(1,128)S(1)} all-to-all(f32[8,1,512]{2,1,0:T(1,128)S(1)} %reshape.496), channel_id=1, replica_groups=mesh['sec'=4,'grp'=8] {'grp'}, dimensions={0} | all-to-all | bytes 32768 | tf_op jit(solution)/shard_map/all_to_all | solution.py:136
  355.5 1.6 reshape.497
  357.2 2.2 copy.177
  359.4 1.6 copy.178
  361.0 12.4 %psum.187 = f32[2,32,2,2,16]{4,1,2,0,3:T(8,128)} all-reduce(f32[2,32,2,2,16]{4,1,2,0,3:T(8,128)} %copy.178), channel_id=1, replica_groups=mesh['sec'=4,'grp'=8] {'sec'}, use_global_device_ids=true, to_apply=%region_32.33 | all-reduce | flops 4096 | bytes 32768 | tf_op jit(solution)/shard_map/psum | solution.py:137
  376.0 1.5 fusion.64
  377.6 1.2 add_multiply_fusion.1
  378.8 2.5 fusion.61
  383.1 8.9 %all_to_all.149 = f32[8,1,512]{2,1,0:T(1,128)S(1)} all-to-all(f32[8,1,512]{2,1,0:T(1,128)S(1)} %reshape.498), channel_id=1, replica_groups=mesh['sec'=4,'grp'=8] {'grp'}, dimensions={0} | all-to-all | bytes 32768 | tf_op jit(solution)/shard_map/all_to_all | solution.py:141
  396.1 10.1 %psum.188 = f32[2,4,2,2,128]{4,3,2,1,0:T(2,128)S(1)} all-reduce(f32[2,4,2,2,128]{4,3,2,1,0:T(2,128)S(1)} %reshape.460), channel_id=1, replica_groups=mesh['sec'=4,'grp'=8] {'sec'}, use_global_device_ids=true, to_apply=%region_33.34 | all-reduce | flops 4096 | bytes 32768 | tf_op jit(solution)/shard_map/psum | solution.py:142
  406.4 2.2 multiply_reduce_fusion.1
  408.7 38.7 %all-reduce = (f32[2]{0:T(128)S(1)}, f32[2]{0:T(128)S(1)}, f32[2]{0:T(128)S(1)}, f32[2]{0:T(128)S(1)}) all-reduce(f32[2]{0:T(128)S(1)} %get-tuple-element.18, f32[2]{0:T(128)S(1)} %get-tuple-element.17, f32[2]{0:T(128)S(1)} %get-tuple-element.16, f32[2]{0:T(128)S(1)} %get-tuple-element.15), channel_id=1, replica_groups=mesh['sec'=4,'grp'=8] {'sec','grp'}, use_global_device_ids=true, to_apply=%region_27.28 | all-reduce | flops 8 | bytes 64 | tf_op jit(solution)/shard_map/psum | solution.py:145
  447.4 1.6 multiply_add_fusion
  (136 shorter events, 51.0 us)
Async XLA Ops:
  0.6 1.9 copy-start
  0.6 14.5 %copy-start.7 = (s32[32]{0:T(128)S(1)}, s32[32]{0:T(128)}, u32[]{:S(2)}) copy-start(s32[32]{0:T(128)} %param.21) | copy-start | bytes 388
  0.7 14.6 %copy-start.8 = (f32[128]{0:T(128)S(1)}, f32[128]{0:T(128)}, u32[]{:S(2)}) copy-start(f32[128]{0:T(128)} %param.20) | copy-start | bytes 1540
  7.9 13.9 %all-to-all-start = ((f32[8,1,512]{2,1,0:T(1,128)}), f32[8,1,512]{2,1,0:T(1,128)S(1)}, u32[]{:S(2)}, u32[]{:S(2)}) async-start(f32[8,1,512]{2,1,0:T(1,128)} %reshape.484), calls=%async_computation | async-start | bytes 32768 | tf_op jit(solution)/shard_map/all_to_all | solution.py:136
  16.6 0.7 copy-start.1
  24.6 31.2 %copy-start.6 = (f32[2,1536]{1,0:T(2,128)S(1)}, f32[2,1536]{1,0:T(2,128)}, u32[]{:S(2)}) copy-start(f32[2,1536]{1,0:T(2,128)} %param.15) | copy-start | bytes 36868
  50.2 11.1 %all-to-all-start.1 = ((f32[8,1,512]{2,1,0:T(1,128)}), f32[8,1,512]{2,1,0:T(1,128)S(1)}, u32[]{:S(2)}, u32[]{:S(2)}) async-start(f32[8,1,512]{2,1,0:T(1,128)} %reshape.486), calls=%async_computation.1 | async-start | bytes 32768 | tf_op jit(solution)/shard_map/all_to_all | solution.py:141
  118.2 0.7 copy-start.2
  228.9 0.7 copy-start.4
  339.4 0.7 copy-start.5
  378.8 68.6 %copy-start.3 = (f32[2,4,4,1536]{3,2,0,1:T(4,128)S(1)}, f32[2,4,4,1536]{3,2,0,1:T(4,128)}, u32[]{:S(2)}) copy-start(f32[2,4,4,1536]{3,2,0,1:T(4,128)} %copy-done.2) | copy-start | bytes 589828
where the time goes:
time: 454 us; the launch traced here: 451 us
  blocking collectives  304 us (67%)
  local copies, waits for them, and re-layouts  67 us (15%)
  matrix products  29.7 us (7%)
  other arithmetic  29.5 us (6%)
  starting transfers between devices  11.8 us (3%)
  waiting for transfers between devices  7.35 us (2%)
    psum x4, blocking collectives, per_device(): lax.psum((totals(residual * residual), totals(direction * image), totals(...  155 us
    psum x4, blocking collectives, per_device(): field = lax.psum(field, 'sec')  49.9 us
    psum x4, blocking collectives, per_device(): folded = lax.psum(folded, 'sec')  40.5 us
    all_to_all x3, blocking collectives, per_device(): lax.all_to_all(apply_field, 'grp', split_axis=3, concat_axis=1, tiled=True)  32.7 us
    unnamed x37, local copies, waits for them, and re-layouts  28.9 us
    all_to_all x3, blocking collectives, per_device(): lax.all_to_all(partial_field, 'grp', split_axis=1, concat_axis=3, tiled=T...  26.8 us
    dot_general x4, matrix products, pixel_segment(): jnp.dot(weighted, table.T, precision=lax.Precision.HIGHEST, preferred_ele...  9.92 us
    all_to_all x5, local copies, waits for them, and re-layouts, per_device(): lax.all_to_all(apply_field, 'grp', split_axis=3, concat_axis=1, tiled=True)  9.38 us
  transfers between devices with their start and end apart: 2, of which 2 were waited for; matrix products, arithmetic and copies ran while one was open for 1% of the time, Pallas kernels for 0%

commit v1 on v0

v1 whole, which is shorter than its diff:
```python
import functools
import math

import jax
import jax.numpy as jnp
from jax import lax
from jax.experimental import pallas as pl
from jax.experimental.pallas import tpu as pltpu
from jax.sharding import PartitionSpec as P

ITERS = 4
LANES = 128
ROWS = 8
full_turn = 2.0 * math.pi
f32 = jnp.float32
bf16 = jnp.bfloat16

to_message = tuple(b * 4 + p * 2 + q for q in (0, 1) for b in (0, 1) for p in (0, 1))
from_message = tuple(to_message.index(n) for n in range(ROWS))
flipped = tuple(n ^ 3 for n in range(ROWS))


def row_index(shape):
    return lax.broadcasted_iota(jnp.int32, shape, 0)


def lane_index(shape):
    return lax.broadcasted_iota(jnp.int32, shape, 1)


def permute_rows(x, order):
    rows = row_index(x.shape)
    by_shift = {}
    for t, n in enumerate(order):
        by_shift.setdefault((t - n) % ROWS, []).append(t)
    out = None
    for shift, targets in by_shift.items():
        moved = pltpu.roll(x, shift, 0) if shift else x
        if out is None:
            out = moved
        else:
            mask = functools.reduce(jnp.logical_or, [rows == t for t in targets])
            out = jnp.where(mask, moved, out)
    return out


def swap_blocks(x):
    width = LANES // ROWS
    rows = row_index(x.shape)
    block = lane_index(x.shape) // width
    for k in (4, 2, 1):
        row_bit = (rows & k) != 0
        block_bit = (block & k) != 0
        down = pltpu.roll(pltpu.roll(x, k, 0), (LANES - k * width) % LANES, 1)
        if k == 4:
            x = jnp.where(row_bit != block_bit, down, x)
        else:
            up = pltpu.roll(pltpu.roll(x, ROWS - k, 0), k * width, 1)
            x = jnp.where(row_bit == block_bit, x, jnp.where(row_bit, down, up))
    return x


def split_rows(x):
    high = x.astype(bf16).astype(f32)
    return jnp.concatenate([high, x - high], axis=0).astype(bf16)


def flip_signed(x):
    rows = row_index(x.shape)
    same = ((rows >> 1) & 1) == (rows & 1)
    moved = permute_rows(x, flipped)
    return jnp.where(same, moved, -moved)


def row_totals(x):
    tile = x[:, :LANES]
    for k in range(1, x.shape[1] // LANES):
        tile = tile + x[:, k * LANES : (k + 1) * LANES]
    rows = row_index(tile.shape)
    first = jnp.sum(jnp.where(rows < 4, tile, 0.0), axis=0, keepdims=True)
    second = jnp.sum(jnp.where(rows < 4, 0.0, tile), axis=0, keepdims=True)
    return join_halves(first, second)


def join_halves(first, second):
    first = first + pltpu.roll(first, LANES // 2, 1)
    second = second + pltpu.roll(second, LANES // 2, 1)
    return jnp.where(lane_index(first.shape) < LANES // 2, first, second)


def pair(vector):
    low = lane_index(vector.shape) < LANES // 2
    return (
        jnp.sum(jnp.where(low, vector, 0.0), axis=1, keepdims=True),
        jnp.sum(jnp.where(low, 0.0, vector), axis=1, keepdims=True),
    )


def by_row(two, shape):
    return jnp.where(row_index(shape) < 4, two[0], two[1])


def by_lane(two, shape):
    quarter = LANES // 4
    return jnp.where((lane_index(shape) // quarter) % 2 == 0, two[0], two[1])


def forward_send(values, legendre_ref, send_ref, m, sections, cycles):
    prod = lax.dot_general(
        split_rows(values),
        legendre_ref[m],
        (((1,), (1,)), ((), ())),
        preferred_element_type=f32,
    )
    prod = prod[:ROWS] + prod[ROWS:]
    field = flip_signed(prod[:, cycles:]) - prod[:, :cycles]
    field = permute_rows(field, to_message)
    groups = send_ref.shape[0] // sections
    for k in range(cycles // LANES):
        tile = swap_blocks(field[:, k * LANES : (k + 1) * LANES])
        for s in range(sections):
            start = s * groups + k * ROWS
            send_ref[start : start + ROWS, 0, m * LANES : (m + 1) * LANES] = tile


def send_scalars(send_ref, vector, slots):
    count = send_ref.shape[0]
    send_ref[:, 0, slots * LANES :] = jnp.broadcast_to(vector, (count, LANES))


def received_scalars(recv_ref, slots):
    return jnp.sum(recv_ref[:, 0, slots * LANES :], axis=0, keepdims=True)


def received_tile(recv_ref, m, k, sections):
    groups = recv_ref.shape[0] // sections
    total = None
    for s in range(sections):
        start = s * groups + k * ROWS
        part = recv_ref[start : start + ROWS, 0, m * LANES : (m + 1) * LANES]
        total = part if total is None else total + part
    return total


def start_kernel(sections, cycles, residual_ref, direction_ref, legendre_ref, send_ref, r_ref, d_ref):
    slots = r_ref.shape[0]
    square = None
    for m in range(slots):
        r = jnp.concatenate([residual_ref[0, m], residual_ref[1, m]], axis=0)
        d = jnp.concatenate([direction_ref[0, m], direction_ref[1, m]], axis=0)
        r_ref[m] = r
        d_ref[m] = d
        square = r * r if square is None else square + r * r
        forward_send(d, legendre_ref, send_ref, m, sections, cycles)
    send_scalars(send_ref, row_totals(square), slots)


def table_kernel(
    slots, m_ref, phase_ref, qq_ref, qu_ref, uu_ref, mask_ref, table_ref, cos_ref, sin_ref, nqq_ref, nqu_ref, nuu_ref
):
    total_m = cos_ref.shape[0]
    count = nqq_ref.shape[1]
    total = count * lax.axis_size("sec")
    groups = total_m // slots
    rows = row_index((ROWS, LANES))
    columns = []
    for m in range(slots):
        for k in range(groups // ROWS):
            column = jnp.zeros((ROWS, LANES), jnp.int32)
            for i in range(ROWS):
                column = jnp.where(rows == i, m_ref[(k * ROWS + i) * slots + m], column)
            columns.append(column)
    column = jnp.concatenate(columns, axis=0)
    value = column.astype(f32)
    weight = jnp.where(column == 0, 1.0, 2.0).astype(f32)
    lanes = lane_index(column.shape)

    me = lax.axis_index("grp")
    width = LANES // ROWS
    phases = phase_ref[pl.ds(me // ROWS, 1), :]
    spot = lane_index(phases.shape)
    moved = pltpu.roll(phases, (ROWS - me % ROWS) % ROWS * width, 1)
    local = jnp.where(spot < width, moved, 0.0)
    for k in (1, 2, 4):
        local = local + pltpu.roll(local, k * width, 1)
    turn = value * local
    cosine = jnp.cos(turn)
    sine = jnp.sin(turn)
    cos_ref[...] = cosine
    sin_ref[...] = jnp.where(lanes < LANES // 2, -sine, sine)

    def wrap(index):
        return index & (total - 1) if total & (total - 1) == 0 else index % total

    step = full_turn / total
    start = lax.axis_index("sec") * count
    fine = wrap(column * lanes).astype(f32) * step
    coarse = wrap(column * (start + lanes * LANES)).astype(f32) * step
    fine_cos, fine_sin = jnp.cos(fine), jnp.sin(fine)
    coarse_cos, coarse_sin = weight * jnp.cos(coarse), weight * jnp.sin(coarse)
    for a in range(count // LANES):
        cos_a = coarse_cos[:, a : a + 1]
        sin_a = coarse_sin[:, a : a + 1]
        block = jnp.concatenate([cos_a * fine_cos - sin_a * fine_sin, -(sin_a * fine_cos + cos_a * fine_sin)], axis=0)
        high = block.astype(bf16)
        low = (block - high.astype(f32)).astype(bf16)
        here = slice(a * LANES, (a + 1) * LANES)
        table_ref[: 2 * total_m, here] = high
        table_ref[2 * total_m : 4 * total_m, here] = low
        table_ref[4 * total_m :, here] = high
    mask = mask_ref[...].astype(f32)
    nqq_ref[...] = mask * qq_ref[...]
    nqu_ref[...] = mask * qu_ref[...]
    nuu_ref[...] = mask * uu_ref[...]


def pixel_kernel(
    sections,
    chunk,
    first,
    recv_ref,
    table_ref,
    cos_ref,
    sin_ref,
    nqq_ref,
    nqu_ref,
    nuu_ref,
    prior_ref,
    r_ref,
    d_ref,
    field_ref,
    rr_ref,
    send_ref,
    field_out,
    rr_out,
    d_out,
):
    total_m = cos_ref.shape[0]
    slots = r_ref.shape[0]
    groups = total_m // slots
    tiles = [received_tile(recv_ref, m, k, sections) for m in range(slots) for k in range(groups // ROWS)]
    field = jnp.concatenate(tiles, axis=0)
    scalars = received_scalars(recv_ref, slots)
    rr_out[...] = scalars
    if not first:
        now, before = pair(scalars), pair(rr_ref[...])
        ratio = tuple(a / b for a, b in zip(now, before))
        field = field + by_lane(ratio, field.shape) * field_ref[...]
    field_out[...] = field
    half = LANES // 2
    cosine, sine = cos_ref[...], sin_ref[...]
    turned = field * cosine + pltpu.roll(field, half, 1) * sine
    modes = jnp.concatenate([turned[:, :half], turned[:, half:]], axis=0)
    high = modes.astype(bf16).astype(f32)
    rows3 = jnp.concatenate([high, high, modes - high], axis=0).astype(bf16)
    count = nqq_ref.shape[1]
    cycles = nqq_ref.shape[0]
    back = None
    curve = [None, None]
    for c in range(count // chunk):
        here = slice(c * chunk, (c + 1) * chunk)
        pixels = lax.dot_general(
            rows3, table_ref[:, here], (((0,), (0,)), ((), ())), preferred_element_type=f32
        )
        nqq, nqu, nuu = nqq_ref[:, here], nqu_ref[:, here], nuu_ref[:, here]
        parts = []
        for b in range(2):
            q = pixels[2 * b * cycles : (2 * b + 1) * cycles]
            u = pixels[(2 * b + 1) * cycles : (2 * b + 2) * cycles]
            wq = nqq * q + nqu * u
            wu = nqu * q + nuu * u
            parts += [wq, wu]
            product = wq * q + wu * u
            curve[b] = product if curve[b] is None else curve[b] + product
        weighted = jnp.concatenate(parts, axis=0)
        high = weighted.astype(bf16).astype(f32)
        both = jnp.concatenate([high, weighted - high], axis=0).astype(bf16)
        part = lax.dot_general(
            table_ref[: 4 * total_m, here], both, (((1,), (1,)), ((), ())), preferred_element_type=f32
        )
        back = part if back is None else back + part
    top = 2 * total_m
    folded = back[:top, :half] + (back[:top, half:] + back[top:, :half])
    folded = jnp.concatenate([folded[:total_m], folded[total_m:]], axis=1)
    out = folded * cosine - pltpu.roll(folded, half, 1) * sine
    for m in range(slots):
        for k in range(groups // ROWS):
            at = (m * (groups // ROWS) + k) * ROWS
            for s in range(sections):
                start = s * groups + k * ROWS
                send_ref[start : start + ROWS, 0, m * LANES : (m + 1) * LANES] = out[at : at + ROWS]

    prior = prior_rows(prior_ref)
    own = None
    for m in range(slots):
        d = d_ref[m]
        if not first:
            d = r_ref[m] + by_row(ratio, (ROWS, LANES))[:, :1] * d
        d_out[m] = d
        product = prior * d * d
        own = product if own is None else own + product

    def fold(x):
        x = jnp.sum(x, axis=0, keepdims=True)
        tile = x[:, :LANES]
        for k in range(1, x.shape[1] // LANES):
            tile = tile + x[:, k * LANES : (k + 1) * LANES]
        return tile

    send_scalars(send_ref, join_halves(fold(curve[0]), fold(curve[1])) + row_totals(own), slots)


def prior_rows(prior_ref):
    e = prior_ref[0:1, :]
    b = prior_ref[1:2, :]
    shape = (ROWS, prior_ref.shape[1])
    return jnp.where((row_index(shape) >> 1) & 1 == 0, jnp.broadcast_to(e, shape), jnp.broadcast_to(b, shape))


def image_step(sections, cycles, recv_ref, rr_ref, prior_ref, legendre_ref, r_ref, d_ref, m, alpha, prior):
    tiles = []
    for k in range(cycles // LANES):
        tiles.append(permute_rows(swap_blocks(received_tile(recv_ref, m, k, sections)), from_message))
    field = jnp.concatenate(tiles, axis=1) if len(tiles) > 1 else tiles[0]
    both = split_rows(jnp.concatenate([-field, flip_signed(field)], axis=1))
    image = jnp.dot(both, legendre_ref[m], preferred_element_type=f32)
    image = (image[:ROWS] + image[ROWS:]) + prior * d_ref[m]
    return r_ref[m] - alpha * image


def step_size(recv_ref, rr_ref, slots):
    curve = pair(received_scalars(recv_ref, slots))
    two = tuple(a / b for a, b in zip(pair(rr_ref[...]), curve))
    return by_row(two, (ROWS, LANES))[:, :1]


def update_kernel(
    sections, cycles, first, recv_ref, rr_ref, prior_ref, legendre_ref, r_ref, d_ref, x_ref, send_ref, r_out, x_out
):
    slots = r_ref.shape[0]
    alpha = step_size(recv_ref, rr_ref, slots)
    prior = prior_rows(prior_ref)
    square = None
    for m in range(slots):
        r = image_step(sections, cycles, recv_ref, rr_ref, prior_ref, legendre_ref, r_ref, d_ref, m, alpha, prior)
        r_out[m] = r
        square = r * r if square is None else square + r * r
        forward_send(r, legendre_ref, send_ref, m, sections, cycles)
        x_out[m] = alpha * d_ref[m] if first else x_ref[m] + alpha * d_ref[m]
    send_scalars(send_ref, row_totals(square), slots)


def last_kernel(
    sections,
    cycles,
    recv_ref,
    rr_ref,
    prior_ref,
    legendre_ref,
    r_ref,
    d_ref,
    x_ref,
    solution_ref,
    send_ref,
    residual_out,
    solution_out,
):
    slots = r_ref.shape[0]
    alpha = step_size(recv_ref, rr_ref, slots)
    prior = prior_rows(prior_ref)
    square = None
    for m in range(slots):
        r = image_step(sections, cycles, recv_ref, rr_ref, prior_ref, legendre_ref, r_ref, d_ref, m, alpha, prior)
        square = r * r if square is None else square + r * r
        x = x_ref[m] + alpha * d_ref[m]
        for b in range(2):
            residual_out[b, m] = r[4 * b : 4 * b + 4]
            solution_out[b, m] = solution_ref[b, m] + x[4 * b : 4 * b + 4]
    send_scalars(send_ref, row_totals(square), 0)


def end_kernel(recv_ref, rr_ref, d_ref, residual_ref, direction_out):
    slots = d_ref.shape[0]
    now, before = pair(received_scalars(recv_ref, 0)), pair(rr_ref[...])
    for b in range(2):
        ratio = now[b] / before[b]
        for m in range(slots):
            direction_out[b, m] = residual_ref[b, m] + ratio * d_ref[m, 4 * b : 4 * b + 4]


def call(kernel, outs, name, limit=32 << 20, smem=()):
    def run(*args):
        vmem = pl.BlockSpec(memory_space=pltpu.VMEM)
        specs = [pl.BlockSpec(memory_space=pltpu.SMEM) if i in smem else vmem for i in range(len(args))]
        return pl.pallas_call(
            kernel,
            out_shape=[jax.ShapeDtypeStruct(shape, dtype) for shape, dtype in outs],
            in_specs=specs,
            out_specs=[vmem] * len(outs),
            compiler_params=pltpu.CompilerParams(vmem_limit_bytes=limit),
            name=name,
        )(*args)

    return run


def per_device(
    solution_in,
    residual_in,
    direction_in,
    legendre,
    inverse_prior,
    noise_qq,
    noise_qu,
    noise_uu,
    pixel_mask,
    cycle_phase,
    m_values,
):
    sections = lax.axis_size("sec")
    devices = sections * lax.axis_size("grp")
    slots, cycles, length = legendre.shape[0], legendre.shape[2], legendre.shape[3]
    total_m = m_values.shape[0]
    count = noise_qq.shape[1]
    table = legendre.reshape(slots, 2 * cycles, length)
    message = ((devices, 1, (slots + 1) * LANES), f32)
    scalars = ((devices, 1, LANES), f32)
    inner = ((slots, ROWS, length), f32)
    outer = (solution_in.shape, f32)
    vector = ((1, LANES), f32)
    field_like = ((total_m, LANES), f32)
    noise_like = (noise_qq.shape, f32)
    chunk = min(512, count)

    def exchange(x):
        return lax.all_to_all(x, ("sec", "grp"), 0, 0, tiled=True)

    send, r, d = call(functools.partial(start_kernel, sections, cycles), [message, inner, inner], "start")(
        residual_in, direction_in, table
    )
    trig, cosine, sine, nqq, nqu, nuu = call(
        functools.partial(table_kernel, slots),
        [((6 * total_m, count), bf16), field_like, field_like, noise_like, noise_like, noise_like],
        "tables",
        smem=(0,),
    )(m_values, cycle_phase.reshape(-1, LANES), noise_qq, noise_qu, noise_uu, pixel_mask)
    field = cosine
    rr = cosine[:1]
    x = r
    for step in range(ITERS):
        first, last = step == 0, step == ITERS - 1
        recv = exchange(send)
        send, field, rr, d = call(
            functools.partial(pixel_kernel, sections, chunk, first), [message, field_like, vector, inner], "pixels"
        )(recv, trig, cosine, sine, nqq, nqu, nuu, inverse_prior, r, d, field, rr)
        recv = exchange(send)
        if last:
            send, residual, solution = call(
                functools.partial(last_kernel, sections, cycles), [scalars, outer, outer], "last"
            )(recv, rr, inverse_prior, table, r, d, x, solution_in)
        else:
            send, r, x = call(
                functools.partial(update_kernel, sections, cycles, first), [message, inner, inner], "update"
            )(recv, rr, inverse_prior, table, r, d, x)
    recv = exchange(send)
    (direction,) = call(end_kernel, [outer], "end")(recv, rr, d, residual)
    return solution, residual, direction


def solution(mesh):
    return jax.shard_map(
        per_device,
        mesh=mesh,
        in_specs=(
            P(None, "grp", None, "sec"),
            P(None, "grp", None, "sec"),
            P(None, "grp", None, "sec"),
            P("grp", None, None, "sec"),
            P(None, "sec"),
            P("grp", "sec"),
            P("grp", "sec"),
            P("grp", "sec"),
            P("grp", "sec"),
            P(),
            P(),
        ),
        out_specs=(
            P(None, "grp", None, "sec"),
            P(None, "grp", None, "sec"),
            P(None, "grp", None, "sec"),
        ),
        check_vma=False,
    )
```

time: 454 us -> 119 us (0.26)
  blocking collectives: 304 us -> 76.6 us
  local copies, waits for them, and re-layouts: 67 us -> 16.8 us
  matrix products: 29.7 us -> 0 us
  other arithmetic: 29.5 us -> 0 us
  Pallas kernels: 0 us -> 17 us
  waiting for transfers between devices: 7.35 us -> 0.01 us
    psum x12 -> x0, blocking collectives: 245 us -> none  [the longest x4 155 us: per_device(): lax.psum((totals(residual * residual), totals(direction * image), totals(...]
    dot_general x16 -> x0, matrix products: 29.7 us -> none  [the longest x4 9.92 us: pixel_segment(): jnp.dot(weighted, table.T, precision=lax.Precision.HIGHEST, preferred_ele...]
    pallas_call x0 -> x11, Pallas kernels: none -> 17 us  [run(): pl.pallas_call(kernel, out_shape=[jax.ShapeDtypeStruct(shape, dtype) for...]
    all_to_all x6 -> x8, blocking collectives: 59.6 us -> 76.6 us  [exchange(): return lax.all_to_all(x, ('sec', 'grp'), 0, 0, tiled=True)]
    all_to_all x13 -> x0, local copies, waits for them, and re-layouts: 15.7 us -> none  [the longest x5 9.38 us: per_device(): lax.all_to_all(apply_field, 'grp', split_axis=3, concat_axis=1, tiled=True)]
    unnamed x37 -> x50, local copies, waits for them, and re-layouts: 28.9 us -> 16.8 us
    reshape x11 -> x0, local copies, waits for them, and re-layouts: 11.7 us -> none  [the longest x3 4.68 us: pixel_segment(): parts = field.reshape(count, modes, 2, 2, cycles)]
    add x13 -> x0, other arithmetic: 7.65 us -> none  [the longest x4 7.42 us: per_device(): residual + (norm_next / norm_now)[:, None, None, None] * direction]
  transfers between devices with their start and end apart: 2 -> 1, of which waited for: 2 -> 0; matrix products, arithmetic and copies ran while one was open for 1% -> 0% of each run, Pallas kernels for 0% -> 1%
where the time goes in v1:
time: 119 us
  blocking collectives  76.6 us (64%)
  Pallas kernels  17 us (14%)
  local copies, waits for them, and re-layouts  16.8 us (14%)
  starting transfers between devices  7.44 us (6%)
    all_to_all x8, blocking collectives, exchange(): return lax.all_to_all(x, ('sec', 'grp'), 0, 0, tiled=True)  76.6 us
    pallas_call x11, Pallas kernels, run(): pl.pallas_call(kernel, out_shape=[jax.ShapeDtypeStruct(shape, dtype) for...  17 us
    unnamed x50, local copies, waits for them, and re-layouts  16.8 us
    all_to_all x1, starting transfers between devices, exchange(): return lax.all_to_all(x, ('sec', 'grp'), 0, 0, tiled=True)  7.44 us
  transfers between devices with their start and end apart: 1, of which 0 were waited for; matrix products, arithmetic and copies ran while one was open for 0% of the time, Pallas kernels for 1%

profile of v1, /device:TPU:0, one launch (start us, length us, event | category | flops | bytes accessed | tf_op | source)
XLA Modules:
  0.0 118.6 jit_solution(6280141485687851924)
XLA Ops:
  0.6 0.0 copy-start.23
  0.6 0.0 copy-start
  0.7 1.9 %copy-done = bf16[4,2,128,1536]{3,2,1,0:T(8,128)(2,1)S(1)} copy-done((bf16[4,2,128,1536]{3,2,1,0:T(8,128)(2,1)S(1)}, bf16[4,2,128,1536]{3,2,1,0:T(8,128)(2,1)}, u32[]{:S(2)}) %copy-start) | copy-done | bytes 3145752
  2.5 0.0 copy-start.14
  2.5 0.9 copy-done.14
  3.5 0.0 copy-start.15
  3.5 0.9 copy-done.15
  4.4 0.0 copy-start.7
  4.4 0.0 copy-start.1
  4.4 1.8 %start.1 = (f32[32,1,640]{2,1,0:T(1,128)}, f32[4,8,1536]{2,1,0:T(8,128)S(1)}, f32[4,8,1536]{2,1,0:T(8,128)S(1)}) custom-call(f32[2,4,4,1536]{3,2,1,0:T(4,128)S(1)} %copy-done.14, f32[2,4,4,1536]{3,2,1,0:T(4,128)S(1)} %copy-done.15, bf16[4,256,1536]{2,1,0:T(8,128)(2,1)S(1)} %bitcast.2), custom_call_target="tpu_custom_call" | custom-call | tf_op jit(solution)/shard_map/start/pallas_call | solution.py:395
  6.2 0.0 copy-start.5
  6.2 0.7 copy-done.5
  6.9 0.0 copy-start.16
  6.9 0.7 copy-done.16
  7.5 7.4 %all-to-all-start = ((f32[32,1,640]{2,1,0:T(1,128)}), f32[32,1,640]{2,1,0:T(1,128)}, u32[]{:S(2)}, u32[]{:S(2)}) async-start(f32[32,1,640]{2,1,0:T(1,128)} %get-tuple-element.39), calls=%async_computation | async-start | bytes 163840 | tf_op jit(solution)/shard_map/all_to_all | solution.py:436
  15.0 0.0 copy-done.23
  15.0 0.0 copy-start.19
  15.0 0.9 copy-done.19
  15.9 0.0 copy-start.20
  15.9 0.9 copy-done.20
  16.8 0.0 copy-start.21
  16.8 0.9 copy-done.21
  17.7 0.0 copy-start.22
  17.7 0.9 copy-done.22
  18.6 0.0 copy-start.24
  18.6 0.7 copy-done.24
  19.3 1.0 tables.1
  20.3 0.0 copy-start.2
  20.3 0.9 copy-done.2
  21.2 0.0 copy-start.10
  21.2 0.6 copy-done.10
  21.8 0.0 copy-start.8
  21.8 0.6 copy-done.8
  22.4 0.0 all-to-all-done.recv_ref
  22.4 0.0 copy-done.7
  22.4 0.0 copy-start.3
  22.4 1.1 copy-done.3
  23.6 0.9 copy-done.6
  24.5 0.7 copy-done.9
  25.2 0.7 copy-done.11
  25.9 0.9 copy-done.17
  26.9 2.2 %pixels.4 = (f32[32,1,640]{2,1,0:T(1,128)S(1)}, f32[32,128]{1,0:T(8,128)S(1)}, f32[1,128]{1,0:T(1,128)S(1)}, f32[4,8,1536]{2,1,0:T(8,128)S(1)}) custom-call(f32[32,1,640]{2,1,0:T(1,128)} %all-to-all-done.recv_ref, bf16[192,2048]{1,0:T(8,128)(2,1)S(1)} %copy-done.3, f32[32,128]{1,0:T(8,128)S(1)} %copy-done.9, f32[32,128]{1,0:T(8,128)S(1)} %copy-done.11, ...), custom_call_target="tpu_custom_call" | custom-call | tf_op jit(solution)/shard_map/pixels/pallas_call | solution.py:395
  29.0 13.0 %all_to_all.45.recv_ref = f32[32,1,640]{2,1,0:T(1,128)S(1)} all-to-all(f32[32,1,640]{2,1,0:T(1,128)S(1)} %get-tuple-element.48), channel_id=1, replica_groups=mesh['sec'=4,'grp'=8] {'sec','grp'}, dimensions={0} | all-to-all | bytes 163840 | tf_op jit(solution)/shard_map/all_to_all | solution.py:436
  42.0 0.0 copy-done.1
  42.0 1.8 %update.3 = (f32[32,1,640]{2,1,0:T(1,128)S(1)}, f32[4,8,1536]{2,1,0:T(8,128)S(1)}, f32[4,8,1536]{2,1,0:T(8,128)S(1)}) custom-call(f32[32,1,640]{2,1,0:T(1,128)S(1)} %all_to_all.45.recv_ref, f32[1,128]{1,0:T(1,128)S(1)} %get-tuple-element.49.rr_ref, f32[2,1536]{1,0:T(2,128)S(1)} %copy-done.7, bf16[4,256,1536]{2,1,0:T(8,128)(2,1)S(1)} %bitcast.3, ...), custom_call_target="tpu_custom_call" | custom-call | tf_op jit(solution)/shard_map/update/pallas_call | solution.py:395
  43.8 9.1 %all_to_all.46.recv_ref = f32[32,1,640]{2,1,0:T(1,128)S(1)} all-to-all(f32[32,1,640]{2,1,0:T(1,128)S(1)} %get-tuple-element.51), channel_id=1, replica_groups=mesh['sec'=4,'grp'=8] {'sec','grp'}, dimensions={0} | all-to-all | bytes 163840 | tf_op jit(solution)/shard_map/all_to_all | solution.py:436
  52.9 0.0 copy-done.4
  52.9 0.0 copy-done.12
  52.9 1.3 %pixels.5 = (f32[32,1,640]{2,1,0:T(1,128)S(1)}, f32[32,128]{1,0:T(8,128)S(1)}, f32[1,128]{1,0:T(1,128)S(1)}, f32[4,8,1536]{2,1,0:T(8,128)S(1)}) custom-call(f32[32,1,640]{2,1,0:T(1,128)S(1)} %all_to_all.46.recv_ref, bf16[192,2048]{1,0:T(8,128)(2,1)S(1)} %copy-done.4, f32[32,128]{1,0:T(8,128)S(1)} %copy-done.9, f32[32,128]{1,0:T(8,128)S(1)} %copy-done.12, ...), custom_call_target="tpu_custom_call" | custom-call | tf_op jit(solution)/shard_map/pixels/pallas_call | solution.py:395
  54.2 9.1 %all_to_all.47.recv_ref = f32[32,1,640]{2,1,0:T(1,128)S(1)} all-to-all(f32[32,1,640]{2,1,0:T(1,128)S(1)} %get-tuple-element.54), channel_id=1, replica_groups=mesh['sec'=4,'grp'=8] {'sec','grp'}, dimensions={0} | all-to-all | bytes 163840 | tf_op jit(solution)/shard_map/all_to_all | solution.py:436
  63.3 1.8 %update.4 = (f32[32,1,640]{2,1,0:T(1,128)S(1)}, f32[4,8,1536]{2,1,0:T(8,128)S(1)}, f32[4,8,1536]{2,1,0:T(8,128)S(1)}) custom-call(f32[32,1,640]{2,1,0:T(1,128)S(1)} %all_to_all.47.recv_ref, f32[1,128]{1,0:T(1,128)S(1)} %get-tuple-element.55.rr_ref, f32[2,1536]{1,0:T(2,128)S(1)} %copy-done.7, bf16[4,256,1536]{2,1,0:T(8,128)(2,1)S(1)} %bitcast.4, ...), custom_call_target="tpu_custom_call" | custom-call | tf_op jit(solution)/shard_map/update/pallas_call | solution.py:395
  65.1 9.1 %all_to_all.48.recv_ref = f32[32,1,640]{2,1,0:T(1,128)S(1)} all-to-all(f32[32,1,640]{2,1,0:T(1,128)S(1)} %get-tuple-element.58), channel_id=1, replica_groups=mesh['sec'=4,'grp'=8] {'sec','grp'}, dimensions={0} | all-to-all | bytes 163840 | tf_op jit(solution)/shard_map/all_to_all | solution.py:436
  74.2 1.3 %pixels.6 = (f32[32,1,640]{2,1,0:T(1,128)S(1)}, f32[32,128]{1,0:T(8,128)S(1)}, f32[1,128]{1,0:T(1,128)S(1)}, f32[4,8,1536]{2,1,0:T(8,128)S(1)}) custom-call(f32[32,1,640]{2,1,0:T(1,128)S(1)} %all_to_all.48.recv_ref, bf16[192,2048]{1,0:T(8,128)(2,1)S(1)} %copy-done.4, f32[32,128]{1,0:T(8,128)S(1)} %copy-done.9, f32[32,128]{1,0:T(8,128)S(1)} %copy-done.12, ...), custom_call_target="tpu_custom_call" | custom-call | tf_op jit(solution)/shard_map/pixels/pallas_call | solution.py:395
  75.5 0.0 copy-start.13
  75.5 9.2 %all_to_all.49.recv_ref = f32[32,1,640]{2,1,0:T(1,128)S(1)} all-to-all(f32[32,1,640]{2,1,0:T(1,128)S(1)} %get-tuple-element.61), channel_id=1, replica_groups=mesh['sec'=4,'grp'=8] {'sec','grp'}, dimensions={0} | all-to-all | bytes 163840 | tf_op jit(solution)/shard_map/all_to_all | solution.py:436
  84.7 1.8 %update.5 = (f32[32,1,640]{2,1,0:T(1,128)S(1)}, f32[4,8,1536]{2,1,0:T(8,128)S(1)}, f32[4,8,1536]{2,1,0:T(8,128)S(1)}) custom-call(f32[32,1,640]{2,1,0:T(1,128)S(1)} %all_to_all.49.recv_ref, f32[1,128]{1,0:T(1,128)S(1)} %get-tuple-element.62.rr_ref, f32[2,1536]{1,0:T(2,128)S(1)} %copy-done.7, bf16[4,256,1536]{2,1,0:T(8,128)(2,1)S(1)} %bitcast.5, ...), custom_call_target="tpu_custom_call" | custom-call | tf_op jit(solution)/shard_map/update/pallas_call | solution.py:395
  86.5 9.1 %all_to_all.50.recv_ref = f32[32,1,640]{2,1,0:T(1,128)S(1)} all-to-all(f32[32,1,640]{2,1,0:T(1,128)S(1)} %get-tuple-element.65), channel_id=1, replica_groups=mesh['sec'=4,'grp'=8] {'sec','grp'}, dimensions={0} | all-to-all | bytes 163840 | tf_op jit(solution)/shard_map/all_to_all | solution.py:436
  95.6 1.8 %pixels.7 = (f32[32,1,640]{2,1,0:T(1,128)S(1)}, f32[32,128]{1,0:T(8,128)}, f32[1,128]{1,0:T(1,128)S(1)}, f32[4,8,1536]{2,1,0:T(8,128)S(1)}) custom-call(f32[32,1,640]{2,1,0:T(1,128)S(1)} %all_to_all.50.recv_ref, bf16[192,2048]{1,0:T(8,128)(2,1)S(1)} %copy-done.4, f32[32,128]{1,0:T(8,128)S(1)} %copy-done.9, f32[32,128]{1,0:T(8,128)S(1)} %copy-done.12, ...), custom_call_target="tpu_custom_call" | custom-call | tf_op jit(solution)/shard_map/pixels/pallas_call | solution.py:395
  97.4 9.1 %all_to_all.51.recv_ref = f32[32,1,640]{2,1,0:T(1,128)S(1)} all-to-all(f32[32,1,640]{2,1,0:T(1,128)S(1)} %get-tuple-element.68), channel_id=1, replica_groups=mesh['sec'=4,'grp'=8] {'sec','grp'}, dimensions={0} | all-to-all | bytes 163840 | tf_op jit(solution)/shard_map/all_to_all | solution.py:436
  106.5 0.0 copy-done.13
  106.5 1.6 %last.1 = (f32[32,1,128]{2,1,0:T(1,128)S(1)}, f32[2,4,4,1536]{3,2,1,0:T(4,128)}, f32[2,4,4,1536]{3,2,1,0:T(4,128)}) custom-call(f32[32,1,640]{2,1,0:T(1,128)S(1)} %all_to_all.51.recv_ref, f32[1,128]{1,0:T(1,128)S(1)} %get-tuple-element.69.rr_ref, f32[2,1536]{1,0:T(2,128)S(1)} %copy-done.7, bf16[4,256,1536]{2,1,0:T(8,128)(2,1)S(1)} %bitcast.6, ...), custom_call_target="tpu_custom_call" | custom-call | tf_op jit(solution)/shard_map/last/pallas_call | solution.py:395
  108.1 8.8 %all_to_all.52.recv_ref = f32[32,1,128]{2,1,0:T(1,128)S(1)} all-to-all(f32[32,1,128]{2,1,0:T(1,128)S(1)} %get-tuple-element.74), channel_id=1, replica_groups=mesh['sec'=4,'grp'=8] {'sec','grp'}, dimensions={0} | all-to-all | bytes 32768 | tf_op jit(solution)/shard_map/all_to_all | solution.py:436
  116.9 0.9 copy-done.18
  117.8 0.8 end.1
  (8 shorter events, 0.0 us)
Async XLA Ops:
  0.6 14.4 %copy-start.23 = (s32[32]{0:T(128)S(1)}, s32[32]{0:T(128)}, u32[]{:S(2)}) copy-start(s32[32]{0:T(128)} %m_ref.1) | copy-start | bytes 388
  0.6 1.9 %copy-start = (bf16[4,2,128,1536]{3,2,1,0:T(8,128)(2,1)S(1)}, bf16[4,2,128,1536]{3,2,1,0:T(8,128)(2,1)}, u32[]{:S(2)}) copy-start(bf16[4,2,128,1536]{3,2,1,0:T(8,128)(2,1)} %param.14) | copy-start | bytes 9437188
  2.5 0.9 copy-start.14
  3.5 0.9 copy-start.15
  4.4 18.0 %copy-start.7 = (f32[2,1536]{1,0:T(2,128)S(1)}, f32[2,1536]{1,0:T(2,128)}, u32[]{:S(2)}) copy-start(f32[2,1536]{1,0:T(2,128)} %prior_ref.15) | copy-start | bytes 36868
  4.4 37.6 %copy-start.1 = (bf16[4,2,128,1536]{3,2,1,0:T(8,128)(2,1)S(1)}, bf16[4,2,128,1536]{3,2,1,0:T(8,128)(2,1)}, u32[]{:S(2)}) copy-start(bf16[4,2,128,1536]{3,2,1,0:T(8,128)(2,1)} %param.14) | copy-start | bytes 9437188
  6.2 0.7 copy-start.5
  6.9 0.7 copy-start.16
  7.5 14.9 %all-to-all-start = ((f32[32,1,640]{2,1,0:T(1,128)}), f32[32,1,640]{2,1,0:T(1,128)}, u32[]{:S(2)}, u32[]{:S(2)}) async-start(f32[32,1,640]{2,1,0:T(1,128)} %get-tuple-element.39), calls=%async_computation | async-start | bytes 163840 | tf_op jit(solution)/shard_map/all_to_all | solution.py:436
  15.0 0.9 copy-start.19
  15.9 0.9 copy-start.20
  16.8 0.9 copy-start.21
  17.7 0.9 copy-start.22
  18.6 0.7 copy-start.24
  20.3 0.9 copy-start.2
  21.2 0.6 copy-start.10
  21.8 0.6 copy-start.8
  22.4 1.1 copy-start.3
  23.6 0.9 copy-start.6
  24.5 0.7 copy-start.9
  25.2 0.7 copy-start.11
  25.9 0.9 copy-start.17
  26.9 26.1 %copy-start.4 = (bf16[192,2048]{1,0:T(8,128)(2,1)S(1)}, bf16[192,2048]{1,0:T(8,128)(2,1)}, u32[]{:S(2)}) copy-start(bf16[192,2048]{1,0:T(8,128)(2,1)} %copy-done.2) | copy-start | bytes 2359300
  26.9 26.1 %copy-start.12 = (f32[32,128]{1,0:T(8,128)S(1)}, f32[32,128]{1,0:T(8,128)}, u32[]{:S(2)}) copy-start(f32[32,128]{1,0:T(8,128)} %copy-done.10) | copy-start | bytes 49156
  75.5 31.0 %copy-start.13 = (f32[2,4,4,1536]{3,2,1,0:T(4,128)S(1)}, f32[2,4,4,1536]{3,2,1,0:T(4,128)}, u32[]{:S(2)}) copy-start(f32[2,4,4,1536]{3,2,1,0:T(4,128)} %solution_ref.1) | copy-start | bytes 589828
  116.9 0.9 copy-start.18

commit v2 on v1

--- a/solution.py
+++ b/solution.py
@@ -142,25 +142,9 @@
     return total
 
 
-def start_kernel(sections, cycles, residual_ref, direction_ref, legendre_ref, send_ref, r_ref, d_ref):
-    slots = r_ref.shape[0]
-    square = None
-    for m in range(slots):
-        r = jnp.concatenate([residual_ref[0, m], residual_ref[1, m]], axis=0)
-        d = jnp.concatenate([direction_ref[0, m], direction_ref[1, m]], axis=0)
-        r_ref[m] = r
-        d_ref[m] = d
-        square = r * r if square is None else square + r * r
-        forward_send(d, legendre_ref, send_ref, m, sections, cycles)
-    send_scalars(send_ref, row_totals(square), slots)
-
-
-def table_kernel(
-    slots, m_ref, phase_ref, qq_ref, qu_ref, uu_ref, mask_ref, table_ref, cos_ref, sin_ref, nqq_ref, nqu_ref, nuu_ref
-):
+def fill_tables(slots, total, m_ref, phase_ref, table_ref, cos_ref, sin_ref):
     total_m = cos_ref.shape[0]
-    count = nqq_ref.shape[1]
-    total = count * lax.axis_size("sec")
+    count = table_ref.shape[1]
     groups = total_m // slots
     rows = row_index((ROWS, LANES))
     columns = []
@@ -208,35 +192,93 @@
         table_ref[: 2 * total_m, here] = high
         table_ref[2 * total_m : 4 * total_m, here] = low
         table_ref[4 * total_m :, here] = high
-    mask = mask_ref[...].astype(f32)
-    nqq_ref[...] = mask * qq_ref[...]
-    nqu_ref[...] = mask * qu_ref[...]
-    nuu_ref[...] = mask * uu_ref[...]
+
+
+def start_kernel(
+    sections,
+    cycles,
+    m_hbm,
+    phase_hbm,
+    residual_hbm,
+    direction_hbm,
+    legendre_hbm,
+    send_ref,
+    table_ref,
+    cos_ref,
+    sin_ref,
+    legendre_ref,
+    r_ref,
+    d_ref,
+    m_ref,
+    phase_ref,
+    residual_ref,
+    direction_ref,
+    small_sems,
+    value_sems,
+    legendre_sems,
+):
+    slots = r_ref.shape[0]
+    small = [
+        pltpu.make_async_copy(m_hbm, m_ref, small_sems.at[0]),
+        pltpu.make_async_copy(phase_hbm, phase_ref, small_sems.at[1]),
+    ]
+    for copy in small:
+        copy.start()
+    copies = [
+        pltpu.make_async_copy(direction_hbm, direction_ref, value_sems.at[0]),
+        pltpu.make_async_copy(residual_hbm, residual_ref, value_sems.at[1]),
+    ]
+    blocks = [
+        pltpu.make_async_copy(legendre_hbm.at[m], legendre_ref.at[m], legendre_sems.at[m]) for m in range(slots)
+    ]
+    copies[0].start()
+    for block in blocks:
+        block.start()
+    copies[1].start()
+    for copy in small:
+        copy.wait()
+    fill_tables(slots, table_ref.shape[1] * sections, m_ref, phase_ref, table_ref, cos_ref, sin_ref)
+    copies[0].wait()
+    for m in range(slots):
+        d = jnp.concatenate([direction_ref[0, m], direction_ref[1, m]], axis=0)
+        d_ref[m] = d
+        blocks[m].wait()
+        forward_send(d, legendre_ref, send_ref, m, sections, cycles)
+    copies[1].wait()
+    square = None
+    for m in range(slots):
+        r = jnp.concatenate([residual_ref[0, m], residual_ref[1, m]], axis=0)
+        r_ref[m] = r
+        square = r * r if square is None else square + r * r
+    send_scalars(send_ref, row_totals(square), slots)
 
 
 def pixel_kernel(
     sections,
     chunk,
     first,
+    last,
     recv_ref,
     table_ref,
     cos_ref,
     sin_ref,
-    nqq_ref,
-    nqu_ref,
-    nuu_ref,
+    qq_ref,
+    qu_ref,
+    uu_ref,
+    mask_ref,
     prior_ref,
-    r_ref,
     d_ref,
-    field_ref,
-    rr_ref,
-    send_ref,
-    field_out,
-    rr_out,
-    d_out,
+    *refs,
 ):
+    if not first:
+        r_ref, field_ref, rr_ref, *refs = refs
+    send_ref, rr_out, *refs = refs
+    if not first:
+        d_out, *refs = refs
+    if not last:
+        (field_out,) = refs
     total_m = cos_ref.shape[0]
-    slots = r_ref.shape[0]
+    slots = d_ref.shape[0]
     groups = total_m // slots
     tiles = [received_tile(recv_ref, m, k, sections) for m in range(slots) for k in range(groups // ROWS)]
     field = jnp.concatenate(tiles, axis=0)
@@ -246,15 +288,16 @@
         now, before = pair(scalars), pair(rr_ref[...])
         ratio = tuple(a / b for a, b in zip(now, before))
         field = field + by_lane(ratio, field.shape) * field_ref[...]
-    field_out[...] = field
+    if not last:
+        field_out[...] = field
     half = LANES // 2
     cosine, sine = cos_ref[...], sin_ref[...]
     turned = field * cosine + pltpu.roll(field, half, 1) * sine
     modes = jnp.concatenate([turned[:, :half], turned[:, half:]], axis=0)
     high = modes.astype(bf16).astype(f32)
     rows3 = jnp.concatenate([high, high, modes - high], axis=0).astype(bf16)
-    count = nqq_ref.shape[1]
-    cycles = nqq_ref.shape[0]
+    count = qq_ref.shape[1]
+    cycles = qq_ref.shape[0]
     back = None
     curve = [None, None]
     for c in range(count // chunk):
@@ -262,7 +305,8 @@
         pixels = lax.dot_general(
             rows3, table_ref[:, here], (((0,), (0,)), ((), ())), preferred_element_type=f32
         )
-        nqq, nqu, nuu = nqq_ref[:, here], nqu_ref[:, here], nuu_ref[:, here]
+        mask = mask_ref[:, here].astype(f32)
+        nqq, nqu, nuu = mask * qq_ref[:, here], mask * qu_ref[:, here], mask * uu_ref[:, here]
         parts = []
         for b in range(2):
             q = pixels[2 * b * cycles : (2 * b + 1) * cycles]
@@ -296,7 +340,7 @@
         d = d_ref[m]
         if not first:
             d = r_ref[m] + by_row(ratio, (ROWS, LANES))[:, :1] * d
-        d_out[m] = d
+            d_out[m] = d
         product = prior * d * d
         own = product if own is None else own + product
 
@@ -335,8 +379,11 @@
 
 
 def update_kernel(
-    sections, cycles, first, recv_ref, rr_ref, prior_ref, legendre_ref, r_ref, d_ref, x_ref, send_ref, r_out, x_out
+    sections, cycles, first, recv_ref, rr_ref, prior_ref, legendre_ref, r_ref, d_ref, *refs
 ):
+    if not first:
+        x_ref, *refs = refs
+    send_ref, r_out, x_out = refs
     slots = r_ref.shape[0]
     alpha = step_size(recv_ref, rr_ref, slots)
     prior = prior_rows(prior_ref)
@@ -364,6 +411,7 @@
     send_ref,
     residual_out,
     solution_out,
+    r_out,
 ):
     slots = r_ref.shape[0]
     alpha = step_size(recv_ref, rr_ref, slots)
@@ -373,30 +421,37 @@
         r = image_step(sections, cycles, recv_ref, rr_ref, prior_ref, legendre_ref, r_ref, d_ref, m, alpha, prior)
         square = r * r if square is None else square + r * r
         x = x_ref[m] + alpha * d_ref[m]
+        r_out[m] = r
         for b in range(2):
             residual_out[b, m] = r[4 * b : 4 * b + 4]
             solution_out[b, m] = solution_ref[b, m] + x[4 * b : 4 * b + 4]
     send_scalars(send_ref, row_totals(square), 0)
 
 
-def end_kernel(recv_ref, rr_ref, d_ref, residual_ref, direction_out):
+def end_kernel(recv_ref, rr_ref, d_ref, r_ref, direction_out):
     slots = d_ref.shape[0]
     now, before = pair(received_scalars(recv_ref, 0)), pair(rr_ref[...])
     for b in range(2):
         ratio = now[b] / before[b]
         for m in range(slots):
-            direction_out[b, m] = residual_ref[b, m] + ratio * d_ref[m, 4 * b : 4 * b + 4]
-
-
-def call(kernel, outs, name, limit=32 << 20, smem=()):
+            here = slice(4 * b, 4 * b + 4)
+            direction_out[b, m] = r_ref[m, here] + ratio * d_ref[m, here]
+
+
+def call(kernel, outs, name, limit=24 << 20, hbm=(), scratch=()):
     def run(*args):
         vmem = pl.BlockSpec(memory_space=pltpu.VMEM)
-        specs = [pl.BlockSpec(memory_space=pltpu.SMEM) if i in smem else vmem for i in range(len(args))]
+        specs = [vmem] * len(args)
+        args = list(args)
+        for i in hbm:
+            specs[i] = pl.BlockSpec(memory_space=pltpu.HBM)
+            args[i] = pltpu.with_memory_space_constraint(args[i], pltpu.HBM)
         return pl.pallas_call(
             kernel,
             out_shape=[jax.ShapeDtypeStruct(shape, dtype) for shape, dtype in outs],
             in_specs=specs,
             out_specs=[vmem] * len(outs),
+            scratch_shapes=list(scratch),
             compiler_params=pltpu.CompilerParams(vmem_limit_bytes=limit),
             name=name,
         )(*args)
@@ -422,48 +477,61 @@
     slots, cycles, length = legendre.shape[0], legendre.shape[2], legendre.shape[3]
     total_m = m_values.shape[0]
     count = noise_qq.shape[1]
-    table = legendre.reshape(slots, 2 * cycles, length)
     message = ((devices, 1, (slots + 1) * LANES), f32)
     scalars = ((devices, 1, LANES), f32)
     inner = ((slots, ROWS, length), f32)
     outer = (solution_in.shape, f32)
     vector = ((1, LANES), f32)
     field_like = ((total_m, LANES), f32)
-    noise_like = (noise_qq.shape, f32)
     chunk = min(512, count)
 
     def exchange(x):
         return lax.all_to_all(x, ("sec", "grp"), 0, 0, tiled=True)
 
-    send, r, d = call(functools.partial(start_kernel, sections, cycles), [message, inner, inner], "start")(
-        residual_in, direction_in, table
-    )
-    trig, cosine, sine, nqq, nqu, nuu = call(
-        functools.partial(table_kernel, slots),
-        [((6 * total_m, count), bf16), field_like, field_like, noise_like, noise_like, noise_like],
-        "tables",
-        smem=(0,),
-    )(m_values, cycle_phase.reshape(-1, LANES), noise_qq, noise_qu, noise_uu, pixel_mask)
-    field = cosine
-    rr = cosine[:1]
-    x = r
+    table = ((6 * total_m, count), bf16)
+    blocks = ((slots, 2 * cycles, length), bf16)
+    send, trig, cosine, sine, rows, r, d = call(
+        functools.partial(start_kernel, sections, cycles),
+        [message, table, field_like, field_like, blocks, inner, inner],
+        "start",
+        hbm=range(5),
+        scratch=(
+            pltpu.SMEM((total_m,), jnp.int32),
+            pltpu.VMEM((cycle_phase.shape[0] // LANES, LANES), f32),
+            pltpu.VMEM(residual_in.shape, f32),
+            pltpu.VMEM(direction_in.shape, f32),
+            pltpu.SemaphoreType.DMA((2,)),
+            pltpu.SemaphoreType.DMA((2,)),
+            pltpu.SemaphoreType.DMA((slots,)),
+        ),
+    )(m_values, cycle_phase.reshape(-1, LANES), residual_in, direction_in, legendre.reshape(blocks[0]))
+    noise = (noise_qq, noise_qu, noise_uu, pixel_mask)
     for step in range(ITERS):
         first, last = step == 0, step == ITERS - 1
         recv = exchange(send)
-        send, field, rr, d = call(
-            functools.partial(pixel_kernel, sections, chunk, first), [message, field_like, vector, inner], "pixels"
-        )(recv, trig, cosine, sine, nqq, nqu, nuu, inverse_prior, r, d, field, rr)
+        carried = () if first else (r, field, rr)
+        out = call(
+            functools.partial(pixel_kernel, sections, chunk, first, last),
+            [message, vector] + ([] if first else [inner]) + ([] if last else [field_like]),
+            "pixels",
+        )(recv, trig, cosine, sine, *noise, inverse_prior, d, *carried)
+        send, rr, *out = out
+        if not first:
+            d, *out = out
+        if not last:
+            (field,) = out
         recv = exchange(send)
+        carried = (recv, rr, inverse_prior, rows, r, d) + (() if first else (x,))
         if last:
-            send, residual, solution = call(
-                functools.partial(last_kernel, sections, cycles), [scalars, outer, outer], "last"
-            )(recv, rr, inverse_prior, table, r, d, x, solution_in)
+            send, residual, solution, r = call(
+                functools.partial(last_kernel, sections, cycles), [scalars, outer, outer, inner], "last"
+            )(*carried, solution_in)
         else:
             send, r, x = call(
                 functools.partial(update_kernel, sections, cycles, first), [message, inner, inner], "update"
-            )(recv, rr, inverse_prior, table, r, d, x)
+            )(*carried)
     recv = exchange(send)
-    (direction,) = call(end_kernel, [outer], "end")(recv, rr, d, residual)
+    (direction,) = call(end_kernel, [outer], "end")(recv, rr, d, r)
     return solution, residual, direction
 
 

time: 119 us -> 106 us (0.89)
  local copies, waits for them, and re-layouts: 16.8 us -> 0.03 us
  blocking collectives: 76.6 us -> 87.3 us
  starting transfers between devices: 7.44 us -> 0 us
    unnamed x50 -> x12, local copies, waits for them, and re-layouts: 16.8 us -> 0.03 us
    all_to_all x8 -> x9, blocking collectives: 76.6 us -> 87.3 us  [exchange(): return lax.all_to_all(x, ('sec', 'grp'), 0, 0, tiled=True)]
    all_to_all x1 -> x0, starting transfers between devices: 7.44 us -> none  [exchange(): return lax.all_to_all(x, ('sec', 'grp'), 0, 0, tiled=True)]
    pallas_call x11 -> x10, Pallas kernels: 17 us -> 17.9 us  [run(): pl.pallas_call(kernel, out_shape=[jax.ShapeDtypeStruct(shape, dtype) for...]
  transfers between devices with their start and end apart: 1 -> 0, of which waited for: 0 -> 0; matrix products, arithmetic and copies ran while one was open for 0% -> 0% of each run, Pallas kernels for 1% -> 0%
where the time goes in v2:
time: 106 us
  blocking collectives  87.3 us (82%)
  Pallas kernels  17.9 us (17%)
    all_to_all x9, blocking collectives, exchange(): return lax.all_to_all(x, ('sec', 'grp'), 0, 0, tiled=True)  87.3 us
    pallas_call x10, Pallas kernels, run(): pl.pallas_call(kernel, out_shape=[jax.ShapeDtypeStruct(shape, dtype) for...  17.9 us

profile of v2, /device:TPU:0, one launch (start us, length us, event | category | flops | bytes accessed | tf_op | source)
XLA Modules:
  0.0 106.0 jit_solution(8026855245055283895)
XLA Ops:
  0.6 0.0 copy-start.4
  0.6 0.0 copy-start.3
  0.7 0.0 copy-start.2
  0.7 0.0 copy-start.1
  0.7 0.0 copy-start
  0.7 5.2 %start.1 = (f32[32,1,640]{2,1,0:T(1,128)S(1)}, bf16[192,2048]{1,0:T(8,128)(2,1)S(1)}, f32[32,128]{1,0:T(8,128)S(1)}, f32[32,128]{1,0:T(8,128)S(1)}, bf16[4,256,1...) custom-call(s32[32]{0:T(128)} %m_hbm.1, f32[1,128]{1,0:T(1,128)} %bitcast.3, ...), custom_call_target="tpu_custom_call" | custom-call | tf_op jit(solution)/shard_map/start/pallas_call | solution.py:449
  5.9 14.5 %all_to_all.45.recv_ref = f32[32,1,640]{2,1,0:T(1,128)S(1)} all-to-all(f32[32,1,640]{2,1,0:T(1,128)S(1)} %get-tuple-element.37), channel_id=1, replica_groups=mesh['sec'=4,'grp'=8] {'sec','grp'}, dimensions={0} | all-to-all | bytes 163840 | tf_op jit(solution)/shard_map/all_to_all | solution.py:489
  20.4 0.0 copy-done.4
  20.4 0.0 copy-done.3
  20.4 0.0 copy-done.2
  20.4 0.0 copy-done.1
  20.4 0.0 copy-done
  20.4 1.2 %pixels.4 = (f32[32,1,640]{2,1,0:T(1,128)S(1)}, f32[1,128]{1,0:T(1,128)S(1)}, f32[32,128]{1,0:T(8,128)S(1)}) custom-call(f32[32,1,640]{2,1,0:T(1,128)S(1)} %all_to_all.45.recv_ref, bf16[192,2048]{1,0:T(8,128)(2,1)S(1)} %get-tuple-element.38.table_ref, f32[32,128]{1,0:T(8,128)S(1)} %get-tuple-element.39.cos_ref, f32[32,128]{1,0:T(8,128)S(1)} %get-tuple-element.40.sin_ref, ...), custom_call_target="tpu_custom_call" | custom-call | tf_op jit(solution)/shard_map/pixels/pallas_call | solution.py:449
  21.6 9.1 %all_to_all.46.recv_ref = f32[32,1,640]{2,1,0:T(1,128)S(1)} all-to-all(f32[32,1,640]{2,1,0:T(1,128)S(1)} %get-tuple-element.42), channel_id=1, replica_groups=mesh['sec'=4,'grp'=8] {'sec','grp'}, dimensions={0} | all-to-all | bytes 163840 | tf_op jit(solution)/shard_map/all_to_all | solution.py:489
  30.8 1.8 %update.3 = (f32[32,1,640]{2,1,0:T(1,128)S(1)}, f32[4,8,1536]{2,1,0:T(8,128)S(1)}, f32[4,8,1536]{2,1,0:T(8,128)S(1)}) custom-call(f32[32,1,640]{2,1,0:T(1,128)S(1)} %all_to_all.46.recv_ref, f32[1,128]{1,0:T(1,128)S(1)} %get-tuple-element.43.rr_ref.refs_2_, f32[2,1536]{1,0:T(2,128)S(1)} %copy-done.4, ...), custom_call_target="tpu_custom_call" | custom-call | tf_op jit(solution)/shard_map/update/pallas_call | solution.py:449
  32.5 9.1 %all_to_all.47.recv_ref = f32[32,1,640]{2,1,0:T(1,128)S(1)} all-to-all(f32[32,1,640]{2,1,0:T(1,128)S(1)} %get-tuple-element.46), channel_id=1, replica_groups=mesh['sec'=4,'grp'=8] {'sec','grp'}, dimensions={0} | all-to-all | bytes 163840 | tf_op jit(solution)/shard_map/all_to_all | solution.py:489
  41.6 1.3 %pixels.5 = (f32[32,1,640]{2,1,0:T(1,128)S(1)}, f32[1,128]{1,0:T(1,128)S(1)}, f32[4,8,1536]{2,1,0:T(8,128)S(1)}, f32[32,128]{1,0:T(8,128)S(1)}) custom-call(f32[32,1,640]{2,1,0:T(1,128)S(1)} %all_to_all.47.recv_ref, bf16[192,2048]{1,0:T(8,128)(2,1)S(1)} %get-tuple-element.38.table_ref, f32[32,128]{1,0:T(8,128)S(1)} %get-tuple-element.39.cos_ref, ...), custom_call_target="tpu_custom_call" | custom-call | tf_op jit(solution)/shard_map/pixels/pallas_call | solution.py:449
  42.9 9.1 %all_to_all.48.recv_ref = f32[32,1,640]{2,1,0:T(1,128)S(1)} all-to-all(f32[32,1,640]{2,1,0:T(1,128)S(1)} %get-tuple-element.49), channel_id=1, replica_groups=mesh['sec'=4,'grp'=8] {'sec','grp'}, dimensions={0} | all-to-all | bytes 163840 | tf_op jit(solution)/shard_map/all_to_all | solution.py:489
  52.0 1.8 %update.4 = (f32[32,1,640]{2,1,0:T(1,128)S(1)}, f32[4,8,1536]{2,1,0:T(8,128)S(1)}, f32[4,8,1536]{2,1,0:T(8,128)S(1)}) custom-call(f32[32,1,640]{2,1,0:T(1,128)S(1)} %all_to_all.48.recv_ref, f32[1,128]{1,0:T(1,128)S(1)} %get-tuple-element.50.rr_ref.refs_2_, f32[2,1536]{1,0:T(2,128)S(1)} %copy-done.4, ...), custom_call_target="tpu_custom_call" | custom-call | tf_op jit(solution)/shard_map/update/pallas_call | solution.py:449
  53.8 9.1 %all_to_all.49.recv_ref = f32[32,1,640]{2,1,0:T(1,128)S(1)} all-to-all(f32[32,1,640]{2,1,0:T(1,128)S(1)} %get-tuple-element.53), channel_id=1, replica_groups=mesh['sec'=4,'grp'=8] {'sec','grp'}, dimensions={0} | all-to-all | bytes 163840 | tf_op jit(solution)/shard_map/all_to_all | solution.py:489
  62.9 1.3 %pixels.6 = (f32[32,1,640]{2,1,0:T(1,128)S(1)}, f32[1,128]{1,0:T(1,128)S(1)}, f32[4,8,1536]{2,1,0:T(8,128)S(1)}, f32[32,128]{1,0:T(8,128)S(1)}) custom-call(f32[32,1,640]{2,1,0:T(1,128)S(1)} %all_to_all.49.recv_ref, bf16[192,2048]{1,0:T(8,128)(2,1)S(1)} %get-tuple-element.38.table_ref, f32[32,128]{1,0:T(8,128)S(1)} %get-tuple-element.39.cos_ref, ...), custom_call_target="tpu_custom_call" | custom-call | tf_op jit(solution)/shard_map/pixels/pallas_call | solution.py:449
  64.2 0.0 copy-start.5
  64.2 9.2 %all_to_all.50.recv_ref = f32[32,1,640]{2,1,0:T(1,128)S(1)} all-to-all(f32[32,1,640]{2,1,0:T(1,128)S(1)} %get-tuple-element.56), channel_id=1, replica_groups=mesh['sec'=4,'grp'=8] {'sec','grp'}, dimensions={0} | all-to-all | bytes 163840 | tf_op jit(solution)/shard_map/all_to_all | solution.py:489
  73.5 1.8 %update.5 = (f32[32,1,640]{2,1,0:T(1,128)S(1)}, f32[4,8,1536]{2,1,0:T(8,128)S(1)}, f32[4,8,1536]{2,1,0:T(8,128)S(1)}) custom-call(f32[32,1,640]{2,1,0:T(1,128)S(1)} %all_to_all.50.recv_ref, f32[1,128]{1,0:T(1,128)S(1)} %get-tuple-element.57.rr_ref.refs_2_, f32[2,1536]{1,0:T(2,128)S(1)} %copy-done.4, ...), custom_call_target="tpu_custom_call" | custom-call | tf_op jit(solution)/shard_map/update/pallas_call | solution.py:449
  75.2 9.1 %all_to_all.51.recv_ref = f32[32,1,640]{2,1,0:T(1,128)S(1)} all-to-all(f32[32,1,640]{2,1,0:T(1,128)S(1)} %get-tuple-element.60), channel_id=1, replica_groups=mesh['sec'=4,'grp'=8] {'sec','grp'}, dimensions={0} | all-to-all | bytes 163840 | tf_op jit(solution)/shard_map/all_to_all | solution.py:489
  84.4 1.3 %pixels.7 = (f32[32,1,640]{2,1,0:T(1,128)S(1)}, f32[1,128]{1,0:T(1,128)S(1)}, f32[4,8,1536]{2,1,0:T(8,128)S(1)}) custom-call(f32[32,1,640]{2,1,0:T(1,128)S(1)} %all_to_all.51.recv_ref, bf16[192,2048]{1,0:T(8,128)(2,1)S(1)} %get-tuple-element.38.table_ref, f32[32,128]{1,0:T(8,128)S(1)} %get-tuple-element.39.cos_ref, f32[32,128]{1,0:T(8,128)S(1)} %get-tuple-element.40.sin_ref, ...), custom_call_target="tpu_custom_call" | custom-call | tf_op jit(solution)/shard_map/pixels/pallas_call | solution.py:449
  85.6 9.1 %all_to_all.52.recv_ref = f32[32,1,640]{2,1,0:T(1,128)S(1)} all-to-all(f32[32,1,640]{2,1,0:T(1,128)S(1)} %get-tuple-element.63), channel_id=1, replica_groups=mesh['sec'=4,'grp'=8] {'sec','grp'}, dimensions={0} | all-to-all | bytes 163840 | tf_op jit(solution)/shard_map/all_to_all | solution.py:489
  94.7 0.0 copy-done.5
  94.7 1.6 %last.1 = (f32[32,1,128]{2,1,0:T(1,128)S(1)}, f32[2,4,4,1536]{3,2,1,0:T(4,128)}, f32[2,4,4,1536]{3,2,1,0:T(4,128)}, f32[4,8,1536]{2,1,0:T(8,128)S(1)}) custom-call(f32[32,1,640]{2,1,0:T(1,128)S(1)} %all_to_all.52.recv_ref, f32[1,128]{1,0:T(1,128)S(1)} %get-tuple-element.64.rr_ref, f32[2,1536]{1,0:T(2,128)S(1)} %copy-done.4, ...), custom_call_target="tpu_custom_call" | custom-call | tf_op jit(solution)/shard_map/last/pallas_call | solution.py:449
  96.3 8.8 %all_to_all.53.recv_ref = f32[32,1,128]{2,1,0:T(1,128)S(1)} all-to-all(f32[32,1,128]{2,1,0:T(1,128)S(1)} %get-tuple-element.69), channel_id=1, replica_groups=mesh['sec'=4,'grp'=8] {'sec','grp'}, dimensions={0} | all-to-all | bytes 32768 | tf_op jit(solution)/shard_map/all_to_all | solution.py:489
  105.1 0.8 end.1
Async XLA Ops:
  0.6 19.8 %copy-start.4 = (f32[2,1536]{1,0:T(2,128)S(1)}, f32[2,1536]{1,0:T(2,128)}, u32[]{:S(2)}) copy-start(f32[2,1536]{1,0:T(2,128)} %prior_ref.15) | copy-start | bytes 36868
  0.6 19.8 %copy-start.3 = (s32[16,2048]{1,0:T(8,128)S(1)}, s32[16,2048]{1,0:T(8,128)}, u32[]{:S(2)}) copy-start(s32[16,2048]{1,0:T(8,128)} %mask_ref.7) | copy-start | bytes 393220
  0.7 19.8 %copy-start.2 = (f32[16,2048]{1,0:T(8,128)S(1)}, f32[16,2048]{1,0:T(8,128)}, u32[]{:S(2)}) copy-start(f32[16,2048]{1,0:T(8,128)} %uu_ref.7) | copy-start | bytes 393220
  0.7 19.8 %copy-start.1 = (f32[16,2048]{1,0:T(8,128)S(1)}, f32[16,2048]{1,0:T(8,128)}, u32[]{:S(2)}) copy-start(f32[16,2048]{1,0:T(8,128)} %qu_ref.7) | copy-start | bytes 393220
  0.7 19.8 %copy-start = (f32[16,2048]{1,0:T(8,128)S(1)}, f32[16,2048]{1,0:T(8,128)}, u32[]{:S(2)}) copy-start(f32[16,2048]{1,0:T(8,128)} %qq_ref.7) | copy-start | bytes 393220
  64.2 30.5 %copy-start.5 = (f32[2,4,4,1536]{3,2,1,0:T(4,128)S(1)}, f32[2,4,4,1536]{3,2,1,0:T(4,128)}, u32[]{:S(2)}) copy-start(f32[2,4,4,1536]{3,2,1,0:T(4,128)} %solution_ref.1) | copy-start | bytes 589828

commit v3 on v2

--- a/solution.py
+++ b/solution.py
@@ -105,39 +105,51 @@
     return jnp.where((lane_index(shape) // quarter) % 2 == 0, two[0], two[1])
 
 
-def forward_send(values, legendre_ref, send_ref, m, sections, cycles):
-    prod = lax.dot_general(
+def forward_product(values, legendre_ref, m):
+    return lax.dot_general(
         split_rows(values),
         legendre_ref[m],
         (((1,), (1,)), ((), ())),
         preferred_element_type=f32,
     )
+
+
+def forward_send(prod, send_ref, m, sections, cycles, slots):
     prod = prod[:ROWS] + prod[ROWS:]
     field = flip_signed(prod[:, cycles:]) - prod[:, :cycles]
     field = permute_rows(field, to_message)
-    groups = send_ref.shape[0] // sections
     for k in range(cycles // LANES):
-        tile = swap_blocks(field[:, k * LANES : (k + 1) * LANES])
-        for s in range(sections):
-            start = s * groups + k * ROWS
-            send_ref[start : start + ROWS, 0, m * LANES : (m + 1) * LANES] = tile
+        send_tile(send_ref, swap_blocks(field[:, k * LANES : (k + 1) * LANES]), m, k, sections, slots)
+
+
+def tile_rows(ref, m, k, s, sections, slots):
+    groups = ref.shape[0] // (slots + 1) // sections
+    return pl.ds((s * groups + k * ROWS) * (slots + 1) + m, ROWS, stride=slots + 1)
+
+
+def send_tile(send_ref, tile, m, k, sections, slots):
+    for s in range(sections):
+        send_ref[tile_rows(send_ref, m, k, s, sections, slots), :] = tile
+
+
+def scalar_rows(ref, slots):
+    count = ref.shape[0] // (slots + 1)
+    return pl.ds(slots, count, stride=slots + 1) if slots else slice(None)
 
 
 def send_scalars(send_ref, vector, slots):
-    count = send_ref.shape[0]
-    send_ref[:, 0, slots * LANES :] = jnp.broadcast_to(vector, (count, LANES))
+    count = send_ref.shape[0] // (slots + 1)
+    send_ref[scalar_rows(send_ref, slots), :] = jnp.broadcast_to(vector, (count, LANES))
 
 
 def received_scalars(recv_ref, slots):
-    return jnp.sum(recv_ref[:, 0, slots * LANES :], axis=0, keepdims=True)
-
-
-def received_tile(recv_ref, m, k, sections):
-    groups = recv_ref.shape[0] // sections
+    return jnp.sum(recv_ref[scalar_rows(recv_ref, slots), :], axis=0, keepdims=True)
+
+
+def received_tile(recv_ref, m, k, sections, slots):
     total = None
     for s in range(sections):
-        start = s * groups + k * ROWS
-        part = recv_ref[start : start + ROWS, 0, m * LANES : (m + 1) * LANES]
+        part = recv_ref[tile_rows(recv_ref, m, k, s, sections, slots), :]
         total = part if total is None else total + part
     return total
 
@@ -186,12 +198,10 @@
         cos_a = coarse_cos[:, a : a + 1]
         sin_a = coarse_sin[:, a : a + 1]
         block = jnp.concatenate([cos_a * fine_cos - sin_a * fine_sin, -(sin_a * fine_cos + cos_a * fine_sin)], axis=0)
-        high = block.astype(bf16)
-        low = (block - high.astype(f32)).astype(bf16)
+        block = block.astype(bf16)
         here = slice(a * LANES, (a + 1) * LANES)
-        table_ref[: 2 * total_m, here] = high
-        table_ref[2 * total_m : 4 * total_m, here] = low
-        table_ref[4 * total_m :, here] = high
+        table_ref[: 2 * total_m, here] = block
+        table_ref[2 * total_m :, here] = block
 
 
 def start_kernel(
@@ -231,19 +241,19 @@
     blocks = [
         pltpu.make_async_copy(legendre_hbm.at[m], legendre_ref.at[m], legendre_sems.at[m]) for m in range(slots)
     ]
-    copies[0].start()
+    for copy in copies:
+        copy.start()
     for block in blocks:
         block.start()
-    copies[1].start()
     for copy in small:
         copy.wait()
     fill_tables(slots, table_ref.shape[1] * sections, m_ref, phase_ref, table_ref, cos_ref, sin_ref)
     copies[0].wait()
+    rows = []
     for m in range(slots):
         d = jnp.concatenate([direction_ref[0, m], direction_ref[1, m]], axis=0)
         d_ref[m] = d
-        blocks[m].wait()
-        forward_send(d, legendre_ref, send_ref, m, sections, cycles)
+        rows.append(d)
     copies[1].wait()
     square = None
     for m in range(slots):
@@ -251,6 +261,10 @@
         r_ref[m] = r
         square = r * r if square is None else square + r * r
     send_scalars(send_ref, row_totals(square), slots)
+    for block in blocks:
+        block.wait()
+    for m in range(slots):
+        forward_send(forward_product(rows[m], legendre_ref, m), send_ref, m, sections, cycles, slots)
 
 
 def pixel_kernel(
@@ -280,7 +294,7 @@
     total_m = cos_ref.shape[0]
     slots = d_ref.shape[0]
     groups = total_m // slots
-    tiles = [received_tile(recv_ref, m, k, sections) for m in range(slots) for k in range(groups // ROWS)]
+    tiles = [received_tile(recv_ref, m, k, sections, slots) for m in range(slots) for k in range(groups // ROWS)]
     field = jnp.concatenate(tiles, axis=0)
     scalars = received_scalars(recv_ref, slots)
     rr_out[...] = scalars
@@ -295,15 +309,15 @@
     turned = field * cosine + pltpu.roll(field, half, 1) * sine
     modes = jnp.concatenate([turned[:, :half], turned[:, half:]], axis=0)
     high = modes.astype(bf16).astype(f32)
-    rows3 = jnp.concatenate([high, high, modes - high], axis=0).astype(bf16)
+    both = jnp.concatenate([high, modes - high], axis=0).astype(bf16)
     count = qq_ref.shape[1]
     cycles = qq_ref.shape[0]
-    back = None
-    curve = [None, None]
+    top = 2 * total_m
+    folded = None
     for c in range(count // chunk):
         here = slice(c * chunk, (c + 1) * chunk)
         pixels = lax.dot_general(
-            rows3, table_ref[:, here], (((0,), (0,)), ((), ())), preferred_element_type=f32
+            both, table_ref[:, here], (((0,), (0,)), ((), ())), preferred_element_type=f32
         )
         mask = mask_ref[:, here].astype(f32)
         nqq, nqu, nuu = mask * qq_ref[:, here], mask * qu_ref[:, here], mask * uu_ref[:, here]
@@ -311,28 +325,21 @@
         for b in range(2):
             q = pixels[2 * b * cycles : (2 * b + 1) * cycles]
             u = pixels[(2 * b + 1) * cycles : (2 * b + 2) * cycles]
-            wq = nqq * q + nqu * u
-            wu = nqu * q + nuu * u
-            parts += [wq, wu]
-            product = wq * q + wu * u
-            curve[b] = product if curve[b] is None else curve[b] + product
-        weighted = jnp.concatenate(parts, axis=0)
-        high = weighted.astype(bf16).astype(f32)
-        both = jnp.concatenate([high, weighted - high], axis=0).astype(bf16)
+            parts += [nqq * q + nqu * u, nqu * q + nuu * u]
+        weighted = jnp.concatenate(parts, axis=0).astype(bf16)
         part = lax.dot_general(
-            table_ref[: 4 * total_m, here], both, (((1,), (1,)), ((), ())), preferred_element_type=f32
+            table_ref[:top, here], weighted, (((1,), (1,)), ((), ())), preferred_element_type=f32
         )
-        back = part if back is None else back + part
-    top = 2 * total_m
-    folded = back[:top, :half] + (back[:top, half:] + back[top:, :half])
+        folded = part if folded is None else folded + part
     folded = jnp.concatenate([folded[:total_m], folded[total_m:]], axis=1)
     out = folded * cosine - pltpu.roll(folded, half, 1) * sine
+    curve = jnp.sum(field * out, axis=0, keepdims=True)
+    first_side = (lane_index(curve.shape) // (half // 2)) % 2 == 0
+    curve = join_halves(jnp.where(first_side, curve, 0.0), jnp.where(first_side, 0.0, curve))
     for m in range(slots):
         for k in range(groups // ROWS):
             at = (m * (groups // ROWS) + k) * ROWS
-            for s in range(sections):
-                start = s * groups + k * ROWS
-                send_ref[start : start + ROWS, 0, m * LANES : (m + 1) * LANES] = out[at : at + ROWS]
+            send_tile(send_ref, out[at : at + ROWS], m, k, sections, slots)
 
     prior = prior_rows(prior_ref)
     own = None
@@ -344,14 +351,7 @@
         product = prior * d * d
         own = product if own is None else own + product
 
-    def fold(x):
-        x = jnp.sum(x, axis=0, keepdims=True)
-        tile = x[:, :LANES]
-        for k in range(1, x.shape[1] // LANES):
-            tile = tile + x[:, k * LANES : (k + 1) * LANES]
-        return tile
-
-    send_scalars(send_ref, join_halves(fold(curve[0]), fold(curve[1])) + row_totals(own), slots)
+    send_scalars(send_ref, curve + row_totals(own), slots)
 
 
 def prior_rows(prior_ref):
@@ -361,12 +361,15 @@
     return jnp.where((row_index(shape) >> 1) & 1 == 0, jnp.broadcast_to(e, shape), jnp.broadcast_to(b, shape))
 
 
-def image_step(sections, cycles, recv_ref, rr_ref, prior_ref, legendre_ref, r_ref, d_ref, m, alpha, prior):
+def image_terms(recv_ref, m, sections, cycles, slots):
     tiles = []
     for k in range(cycles // LANES):
-        tiles.append(permute_rows(swap_blocks(received_tile(recv_ref, m, k, sections)), from_message))
+        tiles.append(permute_rows(swap_blocks(received_tile(recv_ref, m, k, sections, slots)), from_message))
     field = jnp.concatenate(tiles, axis=1) if len(tiles) > 1 else tiles[0]
-    both = split_rows(jnp.concatenate([-field, flip_signed(field)], axis=1))
+    return split_rows(jnp.concatenate([-field, flip_signed(field)], axis=1))
+
+
+def next_residual(both, legendre_ref, r_ref, d_ref, m, alpha, prior):
     image = jnp.dot(both, legendre_ref[m], preferred_element_type=f32)
     image = (image[:ROWS] + image[ROWS:]) + prior * d_ref[m]
     return r_ref[m] - alpha * image
@@ -388,11 +391,12 @@
     alpha = step_size(recv_ref, rr_ref, slots)
     prior = prior_rows(prior_ref)
     square = None
-    for m in range(slots):
-        r = image_step(sections, cycles, recv_ref, rr_ref, prior_ref, legendre_ref, r_ref, d_ref, m, alpha, prior)
+    terms = [image_terms(recv_ref, m, sections, cycles, slots) for m in range(slots)]
+    for m in range(slots):
+        r = next_residual(terms[m], legendre_ref, r_ref, d_ref, m, alpha, prior)
         r_out[m] = r
         square = r * r if square is None else square + r * r
-        forward_send(r, legendre_ref, send_ref, m, sections, cycles)
+        forward_send(forward_product(r, legendre_ref, m), send_ref, m, sections, cycles, slots)
         x_out[m] = alpha * d_ref[m] if first else x_ref[m] + alpha * d_ref[m]
     send_scalars(send_ref, row_totals(square), slots)
 
@@ -417,8 +421,9 @@
     alpha = step_size(recv_ref, rr_ref, slots)
     prior = prior_rows(prior_ref)
     square = None
-    for m in range(slots):
-        r = image_step(sections, cycles, recv_ref, rr_ref, prior_ref, legendre_ref, r_ref, d_ref, m, alpha, prior)
+    terms = [image_terms(recv_ref, m, sections, cycles, slots) for m in range(slots)]
+    for m in range(slots):
+        r = next_residual(terms[m], legendre_ref, r_ref, d_ref, m, alpha, prior)
         square = r * r if square is None else square + r * r
         x = x_ref[m] + alpha * d_ref[m]
         r_out[m] = r
@@ -477,18 +482,19 @@
     slots, cycles, length = legendre.shape[0], legendre.shape[2], legendre.shape[3]
     total_m = m_values.shape[0]
     count = noise_qq.shape[1]
-    message = ((devices, 1, (slots + 1) * LANES), f32)
-    scalars = ((devices, 1, LANES), f32)
+    message = ((devices * (slots + 1), LANES), f32)
+    scalars = ((devices, LANES), f32)
     inner = ((slots, ROWS, length), f32)
     outer = (solution_in.shape, f32)
     vector = ((1, LANES), f32)
     field_like = ((total_m, LANES), f32)
-    chunk = min(512, count)
+    chunk = min(256, count)
 
     def exchange(x):
-        return lax.all_to_all(x, ("sec", "grp"), 0, 0, tiled=True)
-
-    table = ((6 * total_m, count), bf16)
+        blocks = x.reshape(devices, 1, x.size // devices)
+        return lax.all_to_all(blocks, ("sec", "grp"), 0, 0, tiled=True).reshape(x.shape)
+
+    table = ((4 * total_m, count), bf16)
     blocks = ((slots, 2 * cycles, length), bf16)
     send, trig, cosine, sine, rows, r, d = call(
         functools.partial(start_kernel, sections, cycles),

time: 106 us -> 103 us (0.972)
  Pallas kernels: 17.9 us -> 14.5 us
    pallas_call x10, Pallas kernels: 17.9 us -> 14.5 us  [run(): pl.pallas_call(kernel, out_shape=[jax.ShapeDtypeStruct(shape, dtype) for...]
where the time goes in v3:
time: 103 us; the launch traced here: 102 us
  blocking collectives  87.2 us (85%)
  Pallas kernels  14.5 us (14%)
    all_to_all x9, blocking collectives, exchange(): lax.all_to_all(blocks, ('sec', 'grp'), 0, 0, tiled=True).reshape(x.shape)  87.2 us
    pallas_call x10, Pallas kernels, run(): pl.pallas_call(kernel, out_shape=[jax.ShapeDtypeStruct(shape, dtype) for...  14.5 us

profile of v3, /device:TPU:0, one launch (start us, length us, event | category | flops | bytes accessed | tf_op | source)
XLA Modules:
  0.0 102.4 jit_solution(8241778687290189501)
XLA Ops:
  0.6 0.0 copy-start.4
  0.6 0.0 copy-start.3
  0.7 0.0 copy-start.2
  0.7 0.0 copy-start.1
  0.7 0.0 copy-start
  0.7 3.3 %start.1 = (f32[160,128]{1,0:T(8,128)S(1)}, bf16[128,2048]{1,0:T(8,128)(2,1)S(1)}, f32[32,128]{1,0:T(8,128)S(1)}, f32[32,128]{1,0:T(8,128)S(1)}, bf16[4,256,1536...) custom-call(s32[32]{0:T(128)} %m_hbm.1, f32[1,128]{1,0:T(1,128)} %bitcast.41, ...), custom_call_target="tpu_custom_call" | custom-call | tf_op jit(solution)/shard_map/start/pallas_call | solution.py:454
  4.0 14.5 %all_to_all.45 = f32[32,1,640]{2,1,0:T(1,128)S(1)} all-to-all(f32[32,1,640]{2,1,0:T(1,128)S(1)} %bitcast.33), channel_id=1, replica_groups=mesh['sec'=4,'grp'=8] {'sec','grp'}, dimensions={0} | all-to-all | bytes 163840 | tf_op jit(solution)/shard_map/all_to_all | solution.py:495
  18.5 0.0 copy-done.4
  18.5 0.0 copy-done.3
  18.5 0.0 copy-done.2
  18.5 0.0 copy-done.1
  18.5 0.0 copy-done
  18.5 0.8 pixels.4
  19.4 9.1 %all_to_all.46 = f32[32,1,640]{2,1,0:T(1,128)S(1)} all-to-all(f32[32,1,640]{2,1,0:T(1,128)S(1)} %bitcast.37), channel_id=1, replica_groups=mesh['sec'=4,'grp'=8] {'sec','grp'}, dimensions={0} | all-to-all | bytes 163840 | tf_op jit(solution)/shard_map/all_to_all | solution.py:495
  28.5 1.8 %update.3 = (f32[160,128]{1,0:T(8,128)S(1)}, f32[4,8,1536]{2,1,0:T(8,128)S(1)}, f32[4,8,1536]{2,1,0:T(8,128)S(1)}) custom-call(f32[160,128]{1,0:T(8,128)S(1)} %bitcast.29, f32[1,128]{1,0:T(1,128)S(1)} %get-tuple-element.43.rr_ref.refs_2_, f32[2,1536]{1,0:T(2,128)S(1)} %copy-done.4, bf16[4,256,1536]{2,1,0:T(8,128)(2,1)S(1)} %get-tuple-element.44.legendre_ref, ...), custom_call_target="tpu_custom_call" | custom-call | tf_op jit(solution)/shard_map/update/pallas_call | solution.py:454
  30.2 9.1 %all_to_all.47 = f32[32,1,640]{2,1,0:T(1,128)S(1)} all-to-all(f32[32,1,640]{2,1,0:T(1,128)S(1)} %bitcast.36), channel_id=1, replica_groups=mesh['sec'=4,'grp'=8] {'sec','grp'}, dimensions={0} | all-to-all | bytes 163840 | tf_op jit(solution)/shard_map/all_to_all | solution.py:495
  39.3 0.9 pixels.5
  40.2 9.1 %all_to_all.48 = f32[32,1,640]{2,1,0:T(1,128)S(1)} all-to-all(f32[32,1,640]{2,1,0:T(1,128)S(1)} %bitcast.31), channel_id=1, replica_groups=mesh['sec'=4,'grp'=8] {'sec','grp'}, dimensions={0} | all-to-all | bytes 163840 | tf_op jit(solution)/shard_map/all_to_all | solution.py:495
  49.3 1.8 %update.4 = (f32[160,128]{1,0:T(8,128)S(1)}, f32[4,8,1536]{2,1,0:T(8,128)S(1)}, f32[4,8,1536]{2,1,0:T(8,128)S(1)}) custom-call(f32[160,128]{1,0:T(8,128)S(1)} %bitcast.27, f32[1,128]{1,0:T(1,128)S(1)} %get-tuple-element.50.rr_ref.refs_2_, f32[2,1536]{1,0:T(2,128)S(1)} %copy-done.4, bf16[4,256,1536]{2,1,0:T(8,128)(2,1)S(1)} %get-tuple-element.44.legendre_ref, ...), custom_call_target="tpu_custom_call" | custom-call | tf_op jit(solution)/shard_map/update/pallas_call | solution.py:454
  51.1 9.1 %all_to_all.49 = f32[32,1,640]{2,1,0:T(1,128)S(1)} all-to-all(f32[32,1,640]{2,1,0:T(1,128)S(1)} %bitcast.34), channel_id=1, replica_groups=mesh['sec'=4,'grp'=8] {'sec','grp'}, dimensions={0} | all-to-all | bytes 163840 | tf_op jit(solution)/shard_map/all_to_all | solution.py:495
  60.2 0.9 pixels.6
  61.1 0.0 copy-start.5
  61.1 9.2 %all_to_all.50 = f32[32,1,640]{2,1,0:T(1,128)S(1)} all-to-all(f32[32,1,640]{2,1,0:T(1,128)S(1)} %bitcast.32), channel_id=1, replica_groups=mesh['sec'=4,'grp'=8] {'sec','grp'}, dimensions={0} | all-to-all | bytes 163840 | tf_op jit(solution)/shard_map/all_to_all | solution.py:495
  70.3 1.8 %update.5 = (f32[160,128]{1,0:T(8,128)S(1)}, f32[4,8,1536]{2,1,0:T(8,128)S(1)}, f32[4,8,1536]{2,1,0:T(8,128)S(1)}) custom-call(f32[160,128]{1,0:T(8,128)S(1)} %bitcast.28, f32[1,128]{1,0:T(1,128)S(1)} %get-tuple-element.57.rr_ref.refs_2_, f32[2,1536]{1,0:T(2,128)S(1)} %copy-done.4, bf16[4,256,1536]{2,1,0:T(8,128)(2,1)S(1)} %get-tuple-element.44.legendre_ref, ...), custom_call_target="tpu_custom_call" | custom-call | tf_op jit(solution)/shard_map/update/pallas_call | solution.py:454
  72.1 9.1 %all_to_all.51 = f32[32,1,640]{2,1,0:T(1,128)S(1)} all-to-all(f32[32,1,640]{2,1,0:T(1,128)S(1)} %bitcast.35), channel_id=1, replica_groups=mesh['sec'=4,'grp'=8] {'sec','grp'}, dimensions={0} | all-to-all | bytes 163840 | tf_op jit(solution)/shard_map/all_to_all | solution.py:495
  81.2 0.9 pixels.7
  82.1 9.1 %all_to_all.52 = f32[32,1,640]{2,1,0:T(1,128)S(1)} all-to-all(f32[32,1,640]{2,1,0:T(1,128)S(1)} %bitcast.30), channel_id=1, replica_groups=mesh['sec'=4,'grp'=8] {'sec','grp'}, dimensions={0} | all-to-all | bytes 163840 | tf_op jit(solution)/shard_map/all_to_all | solution.py:495
  91.2 0.0 copy-done.5
  91.2 1.6 %last.1 = (f32[32,128]{1,0:T(8,128)S(1)}, f32[2,4,4,1536]{3,2,1,0:T(4,128)}, f32[2,4,4,1536]{3,2,1,0:T(4,128)}, f32[4,8,1536]{2,1,0:T(8,128)S(1)}) custom-call(f32[160,128]{1,0:T(8,128)S(1)} %bitcast.26, f32[1,128]{1,0:T(1,128)S(1)} %get-tuple-element.64.rr_ref, f32[2,1536]{1,0:T(2,128)S(1)} %copy-done.4, ...), custom_call_target="tpu_custom_call" | custom-call | tf_op jit(solution)/shard_map/last/pallas_call | solution.py:454
  92.8 8.8 %all_to_all.53 = f32[32,1,128]{2,1,0:T(1,128)S(1)} all-to-all(f32[32,1,128]{2,1,0:T(1,128)S(1)} %bitcast.39), channel_id=1, replica_groups=mesh['sec'=4,'grp'=8] {'sec','grp'}, dimensions={0} | all-to-all | bytes 32768 | tf_op jit(solution)/shard_map/all_to_all | solution.py:495
  101.6 0.8 end.1
Async XLA Ops:
  0.6 17.9 %copy-start.4 = (f32[2,1536]{1,0:T(2,128)S(1)}, f32[2,1536]{1,0:T(2,128)}, u32[]{:S(2)}) copy-start(f32[2,1536]{1,0:T(2,128)} %prior_ref.15) | copy-start | bytes 36868
  0.6 17.9 %copy-start.3 = (s32[16,2048]{1,0:T(8,128)S(1)}, s32[16,2048]{1,0:T(8,128)}, u32[]{:S(2)}) copy-start(s32[16,2048]{1,0:T(8,128)} %mask_ref.7) | copy-start | bytes 393220
  0.7 17.9 %copy-start.2 = (f32[16,2048]{1,0:T(8,128)S(1)}, f32[16,2048]{1,0:T(8,128)}, u32[]{:S(2)}) copy-start(f32[16,2048]{1,0:T(8,128)} %uu_ref.7) | copy-start | bytes 393220
  0.7 17.9 %copy-start.1 = (f32[16,2048]{1,0:T(8,128)S(1)}, f32[16,2048]{1,0:T(8,128)}, u32[]{:S(2)}) copy-start(f32[16,2048]{1,0:T(8,128)} %qu_ref.7) | copy-start | bytes 393220
  0.7 17.9 %copy-start = (f32[16,2048]{1,0:T(8,128)S(1)}, f32[16,2048]{1,0:T(8,128)}, u32[]{:S(2)}) copy-start(f32[16,2048]{1,0:T(8,128)} %qq_ref.7) | copy-start | bytes 393220
  61.1 30.1 %copy-start.5 = (f32[2,4,4,1536]{3,2,1,0:T(4,128)S(1)}, f32[2,4,4,1536]{3,2,1,0:T(4,128)}, u32[]{:S(2)}) copy-start(f32[2,4,4,1536]{3,2,1,0:T(4,128)} %solution_ref.1) | copy-start | bytes 589828

commit v4 on v3

--- a/solution.py
+++ b/solution.py
@@ -15,8 +15,6 @@
 f32 = jnp.float32
 bf16 = jnp.bfloat16
 
-to_message = tuple(b * 4 + p * 2 + q for q in (0, 1) for b in (0, 1) for p in (0, 1))
-from_message = tuple(to_message.index(n) for n in range(ROWS))
 flipped = tuple(n ^ 3 for n in range(ROWS))
 
 
@@ -44,20 +42,32 @@
     return out
 
 
-def swap_blocks(x):
+def turn_blocks(buffer_ref, start, stride, distance):
     width = LANES // ROWS
+    out = None
+    for k in range(ROWS):
+        moved = buffer_ref[pl.ds(start + 4 * k, ROWS, stride=stride), :]
+        out = moved if out is None else jnp.where(distance == k, pltpu.roll(moved, k * width, 1), out)
+    return out
+
+
+def store_copies(x, buffer_ref, starts, stride):
+    for start in starts:
+        buffer_ref[pl.ds(start, ROWS, stride=stride), :] = x
+
+
+def to_rows(x, buffer_ref):
+    store_copies(x, buffer_ref, (16, 48, 2, 34), 4)
     rows = row_index(x.shape)
-    block = lane_index(x.shape) // width
-    for k in (4, 2, 1):
-        row_bit = (rows & k) != 0
-        block_bit = (block & k) != 0
-        down = pltpu.roll(pltpu.roll(x, k, 0), (LANES - k * width) % LANES, 1)
-        if k == 4:
-            x = jnp.where(row_bit != block_bit, down, x)
-        else:
-            up = pltpu.roll(pltpu.roll(x, ROWS - k, 0), k * width, 1)
-            x = jnp.where(row_bit == block_bit, x, jnp.where(row_bit, down, up))
-    return x
+    place = (rows & 1) * 4 + (rows >> 1)
+    distance = (lane_index(x.shape) // (LANES // ROWS) - place) & (ROWS - 1)
+    return turn_blocks(buffer_ref, 16, 2, distance)
+
+
+def to_message(x, buffer_ref):
+    store_copies(x, buffer_ref, (0, 14, 32, 46), 2)
+    distance = (lane_index(x.shape) // (LANES // ROWS) - row_index(x.shape)) & (ROWS - 1)
+    return turn_blocks(buffer_ref, 0, 4, distance)
 
 
 def split_rows(x):
@@ -114,12 +124,13 @@
     )
 
 
-def forward_send(prod, send_ref, m, sections, cycles, slots):
+def forward_send(prod, send_ref, buffer_ref, m, sections, cycles, slots):
     prod = prod[:ROWS] + prod[ROWS:]
     field = flip_signed(prod[:, cycles:]) - prod[:, :cycles]
-    field = permute_rows(field, to_message)
     for k in range(cycles // LANES):
-        send_tile(send_ref, swap_blocks(field[:, k * LANES : (k + 1) * LANES]), m, k, sections, slots)
+        tile = field[:, k * LANES : (k + 1) * LANES]
+        at = m * (cycles // LANES) + k
+        send_tile(send_ref, to_message(tile, buffer_ref.at[at]), m, k, sections, slots)
 
 
 def tile_rows(ref, m, k, s, sections, slots):
@@ -223,6 +234,7 @@
     phase_ref,
     residual_ref,
     direction_ref,
+    buffer_ref,
     small_sems,
     value_sems,
     legendre_sems,
@@ -264,7 +276,7 @@
     for block in blocks:
         block.wait()
     for m in range(slots):
-        forward_send(forward_product(rows[m], legendre_ref, m), send_ref, m, sections, cycles, slots)
+        forward_send(forward_product(rows[m], legendre_ref, m), send_ref, buffer_ref, m, sections, cycles, slots)
 
 
 def pixel_kernel(
@@ -361,10 +373,12 @@
     return jnp.where((row_index(shape) >> 1) & 1 == 0, jnp.broadcast_to(e, shape), jnp.broadcast_to(b, shape))
 
 
-def image_terms(recv_ref, m, sections, cycles, slots):
+def image_terms(recv_ref, buffer_ref, m, sections, cycles, slots):
     tiles = []
     for k in range(cycles // LANES):
-        tiles.append(permute_rows(swap_blocks(received_tile(recv_ref, m, k, sections, slots)), from_message))
+        at = m * (cycles // LANES) + k
+        tile = received_tile(recv_ref, m, k, sections, slots)
+        tiles.append(to_rows(tile, buffer_ref.at[at]))
     field = jnp.concatenate(tiles, axis=1) if len(tiles) > 1 else tiles[0]
     return split_rows(jnp.concatenate([-field, flip_signed(field)], axis=1))
 
@@ -386,17 +400,17 @@
 ):
     if not first:
         x_ref, *refs = refs
-    send_ref, r_out, x_out = refs
+    send_ref, r_out, x_out, buffer_ref = refs
     slots = r_ref.shape[0]
     alpha = step_size(recv_ref, rr_ref, slots)
     prior = prior_rows(prior_ref)
     square = None
-    terms = [image_terms(recv_ref, m, sections, cycles, slots) for m in range(slots)]
+    terms = [image_terms(recv_ref, buffer_ref, m, sections, cycles, slots) for m in range(slots)]
     for m in range(slots):
         r = next_residual(terms[m], legendre_ref, r_ref, d_ref, m, alpha, prior)
         r_out[m] = r
         square = r * r if square is None else square + r * r
-        forward_send(forward_product(r, legendre_ref, m), send_ref, m, sections, cycles, slots)
+        forward_send(forward_product(r, legendre_ref, m), send_ref, buffer_ref, m, sections, cycles, slots)
         x_out[m] = alpha * d_ref[m] if first else x_ref[m] + alpha * d_ref[m]
     send_scalars(send_ref, row_totals(square), slots)
 
@@ -415,35 +429,51 @@
     send_ref,
     residual_out,
     solution_out,
-    r_out,
+    buffer_ref,
 ):
     slots = r_ref.shape[0]
     alpha = step_size(recv_ref, rr_ref, slots)
     prior = prior_rows(prior_ref)
+    for m in range(slots):
+        x = x_ref[m] + alpha * d_ref[m]
+        for b in range(2):
+            solution_out[b, m] = solution_ref[b, m] + x[4 * b : 4 * b + 4]
     square = None
-    terms = [image_terms(recv_ref, m, sections, cycles, slots) for m in range(slots)]
+    terms = [image_terms(recv_ref, buffer_ref, m, sections, cycles, slots) for m in range(slots)]
     for m in range(slots):
         r = next_residual(terms[m], legendre_ref, r_ref, d_ref, m, alpha, prior)
         square = r * r if square is None else square + r * r
-        x = x_ref[m] + alpha * d_ref[m]
-        r_out[m] = r
         for b in range(2):
             residual_out[b, m] = r[4 * b : 4 * b + 4]
-            solution_out[b, m] = solution_ref[b, m] + x[4 * b : 4 * b + 4]
     send_scalars(send_ref, row_totals(square), 0)
 
 
-def end_kernel(recv_ref, rr_ref, d_ref, r_ref, direction_out):
+def end_kernel(
+    recv_ref, rr_ref, d_ref, residual_ref, solution_ref, direction_hbm, residual_hbm, solution_hbm, direction_ref, sems
+):
     slots = d_ref.shape[0]
+    copies = [
+        pltpu.make_async_copy(residual_ref, residual_hbm, sems.at[0]),
+        pltpu.make_async_copy(solution_ref, solution_hbm, sems.at[1]),
+        pltpu.make_async_copy(direction_ref, direction_hbm, sems.at[2]),
+    ]
+    copies[0].start()
+    copies[1].start()
     now, before = pair(received_scalars(recv_ref, 0)), pair(rr_ref[...])
-    for b in range(2):
-        ratio = now[b] / before[b]
-        for m in range(slots):
-            here = slice(4 * b, 4 * b + 4)
-            direction_out[b, m] = r_ref[m, here] + ratio * d_ref[m, here]
-
-
-def call(kernel, outs, name, limit=24 << 20, hbm=(), scratch=()):
+    ratios = [now[b] / before[b] for b in range(2)]
+
+    def fill(m, carry):
+        for b in range(2):
+            direction_ref[b, m] = residual_ref[b, m] + ratios[b] * d_ref[m, 4 * b : 4 * b + 4]
+        return carry
+
+    lax.fori_loop(0, slots, fill, 0)
+    copies[2].start()
+    for copy in copies:
+        copy.wait()
+
+
+def call(kernel, outs, name, limit=24 << 20, hbm=(), scratch=(), hbm_outs=()):
     def run(*args):
         vmem = pl.BlockSpec(memory_space=pltpu.VMEM)
         specs = [vmem] * len(args)
@@ -455,7 +485,7 @@
             kernel,
             out_shape=[jax.ShapeDtypeStruct(shape, dtype) for shape, dtype in outs],
             in_specs=specs,
-            out_specs=[vmem] * len(outs),
+            out_specs=[pl.BlockSpec(memory_space=pltpu.HBM) if i in hbm_outs else vmem for i in range(len(outs))],
             scratch_shapes=list(scratch),
             compiler_params=pltpu.CompilerParams(vmem_limit_bytes=limit),
             name=name,
@@ -490,6 +520,8 @@
     field_like = ((total_m, LANES), f32)
     chunk = min(256, count)
 
+    buffers = (pltpu.VMEM((slots * (cycles // LANES), 10 * ROWS, LANES), f32),)
+
     def exchange(x):
         blocks = x.reshape(devices, 1, x.size // devices)
         return lax.all_to_all(blocks, ("sec", "grp"), 0, 0, tiled=True).reshape(x.shape)
@@ -506,6 +538,7 @@
             pltpu.VMEM((cycle_phase.shape[0] // LANES, LANES), f32),
             pltpu.VMEM(residual_in.shape, f32),
             pltpu.VMEM(direction_in.shape, f32),
+            *buffers,
             pltpu.SemaphoreType.DMA((2,)),
             pltpu.SemaphoreType.DMA((2,)),
             pltpu.SemaphoreType.DMA((slots,)),
@@ -529,15 +562,24 @@
         recv = exchange(send)
         carried = (recv, rr, inverse_prior, rows, r, d) + (() if first else (x,))
         if last:
-            send, residual, solution, r = call(
-                functools.partial(last_kernel, sections, cycles), [scalars, outer, outer, inner], "last"
+            send, residual, solution = call(
+                functools.partial(last_kernel, sections, cycles),
+                [scalars, outer, outer],
+                "last",
+                scratch=buffers,
             )(*carried, solution_in)
         else:
             send, r, x = call(
-                functools.partial(update_kernel, sections, cycles, first), [message, inner, inner], "update"
+                functools.partial(update_kernel, sections, cycles, first), [message, inner, inner], "update", scratch=buffers
             )(*carried)
     recv = exchange(send)
-    (direction,) = call(end_kernel, [outer], "end")(recv, rr, d, r)
+    direction, residual, solution = call(
+        end_kernel,
+        [outer, outer, outer],
+        "end",
+        hbm_outs=(0, 1, 2),
+        scratch=(pltpu.VMEM(outer[0], f32), pltpu.SemaphoreType.DMA((3,))),
+    )(recv, rr, d, residual, solution)
     return solution, residual, direction
 
 

time: 103 us -> 101 us (0.981)
  Pallas kernels: 14.5 us -> 12.7 us
    pallas_call x10, Pallas kernels: 14.5 us -> 12.7 us  [run(): pl.pallas_call(kernel, out_shape=[jax.ShapeDtypeStruct(shape, dtype) for...]
where the time goes in v4:
time: 101 us
  blocking collectives  87.2 us (86%)
  Pallas kernels  12.7 us (13%)
    all_to_all x9, blocking collectives, exchange(): lax.all_to_all(blocks, ('sec', 'grp'), 0, 0, tiled=True).reshape(x.shape)  87.2 us
    pallas_call x10, Pallas kernels, run(): pl.pallas_call(kernel, out_shape=[jax.ShapeDtypeStruct(shape, dtype) for...  12.7 us

profile of v4, /device:TPU:0, one launch (start us, length us, event | category | flops | bytes accessed | tf_op | source)
XLA Modules:
  0.0 100.7 jit_solution(13870835709898802992)
XLA Ops:
  0.6 0.0 copy-start.4
  0.6 0.0 copy-start.3
  0.7 0.0 copy-start.2
  0.7 0.0 copy-start.1
  0.7 0.0 copy-start
  0.7 3.2 %start.1 = (f32[160,128]{1,0:T(8,128)S(1)}, bf16[128,2048]{1,0:T(8,128)(2,1)S(1)}, f32[32,128]{1,0:T(8,128)S(1)}, f32[32,128]{1,0:T(8,128)S(1)}, bf16[4,256,1536...) custom-call(s32[32]{0:T(128)} %m_hbm.1, f32[1,128]{1,0:T(1,128)} %bitcast.41, ...), custom_call_target="tpu_custom_call" | custom-call | tf_op jit(solution)/shard_map/start/pallas_call | solution.py:484
  3.8 14.5 %all_to_all.45 = f32[32,1,640]{2,1,0:T(1,128)S(1)} all-to-all(f32[32,1,640]{2,1,0:T(1,128)S(1)} %bitcast.33), channel_id=1, replica_groups=mesh['sec'=4,'grp'=8] {'sec','grp'}, dimensions={0} | all-to-all | bytes 163840 | tf_op jit(solution)/shard_map/all_to_all | solution.py:527
  18.4 0.0 copy-done.4
  18.4 0.0 copy-done.3
  18.4 0.0 copy-done.2
  18.4 0.0 copy-done.1
  18.4 0.0 copy-done
  18.4 0.8 pixels.4
  19.2 9.1 %all_to_all.46 = f32[32,1,640]{2,1,0:T(1,128)S(1)} all-to-all(f32[32,1,640]{2,1,0:T(1,128)S(1)} %bitcast.37), channel_id=1, replica_groups=mesh['sec'=4,'grp'=8] {'sec','grp'}, dimensions={0} | all-to-all | bytes 163840 | tf_op jit(solution)/shard_map/all_to_all | solution.py:527
  28.3 1.5 %update.3 = (f32[160,128]{1,0:T(8,128)S(1)}, f32[4,8,1536]{2,1,0:T(8,128)S(1)}, f32[4,8,1536]{2,1,0:T(8,128)S(1)}) custom-call(f32[160,128]{1,0:T(8,128)S(1)} %bitcast.29, f32[1,128]{1,0:T(1,128)S(1)} %get-tuple-element.45.rr_ref.refs_2_, f32[2,1536]{1,0:T(2,128)S(1)} %copy-done.4, bf16[4,256,1536]{2,1,0:T(8,128)(2,1)S(1)} %get-tuple-element.46.legendre_ref, ...), custom_call_target="tpu_custom_call" | custom-call | tf_op jit(solution)/shard_map/update/pallas_call | solution.py:484
  29.9 9.1 %all_to_all.47 = f32[32,1,640]{2,1,0:T(1,128)S(1)} all-to-all(f32[32,1,640]{2,1,0:T(1,128)S(1)} %bitcast.36), channel_id=1, replica_groups=mesh['sec'=4,'grp'=8] {'sec','grp'}, dimensions={0} | all-to-all | bytes 163840 | tf_op jit(solution)/shard_map/all_to_all | solution.py:527
  39.0 0.9 pixels.5
  39.9 9.1 %all_to_all.48 = f32[32,1,640]{2,1,0:T(1,128)S(1)} all-to-all(f32[32,1,640]{2,1,0:T(1,128)S(1)} %bitcast.31), channel_id=1, replica_groups=mesh['sec'=4,'grp'=8] {'sec','grp'}, dimensions={0} | all-to-all | bytes 163840 | tf_op jit(solution)/shard_map/all_to_all | solution.py:527
  49.0 1.5 %update.4 = (f32[160,128]{1,0:T(8,128)S(1)}, f32[4,8,1536]{2,1,0:T(8,128)S(1)}, f32[4,8,1536]{2,1,0:T(8,128)S(1)}) custom-call(f32[160,128]{1,0:T(8,128)S(1)} %bitcast.27, f32[1,128]{1,0:T(1,128)S(1)} %get-tuple-element.52.rr_ref.refs_2_, f32[2,1536]{1,0:T(2,128)S(1)} %copy-done.4, bf16[4,256,1536]{2,1,0:T(8,128)(2,1)S(1)} %get-tuple-element.46.legendre_ref, ...), custom_call_target="tpu_custom_call" | custom-call | tf_op jit(solution)/shard_map/update/pallas_call | solution.py:484
  50.5 9.1 %all_to_all.49 = f32[32,1,640]{2,1,0:T(1,128)S(1)} all-to-all(f32[32,1,640]{2,1,0:T(1,128)S(1)} %bitcast.34), channel_id=1, replica_groups=mesh['sec'=4,'grp'=8] {'sec','grp'}, dimensions={0} | all-to-all | bytes 163840 | tf_op jit(solution)/shard_map/all_to_all | solution.py:527
  59.6 0.9 pixels.6
  60.5 0.0 copy-start.5
  60.5 9.2 %all_to_all.50 = f32[32,1,640]{2,1,0:T(1,128)S(1)} all-to-all(f32[32,1,640]{2,1,0:T(1,128)S(1)} %bitcast.32), channel_id=1, replica_groups=mesh['sec'=4,'grp'=8] {'sec','grp'}, dimensions={0} | all-to-all | bytes 163840 | tf_op jit(solution)/shard_map/all_to_all | solution.py:527
  69.7 1.5 %update.5 = (f32[160,128]{1,0:T(8,128)S(1)}, f32[4,8,1536]{2,1,0:T(8,128)S(1)}, f32[4,8,1536]{2,1,0:T(8,128)S(1)}) custom-call(f32[160,128]{1,0:T(8,128)S(1)} %bitcast.28, f32[1,128]{1,0:T(1,128)S(1)} %get-tuple-element.59.rr_ref.refs_2_, f32[2,1536]{1,0:T(2,128)S(1)} %copy-done.4, bf16[4,256,1536]{2,1,0:T(8,128)(2,1)S(1)} %get-tuple-element.46.legendre_ref, ...), custom_call_target="tpu_custom_call" | custom-call | tf_op jit(solution)/shard_map/update/pallas_call | solution.py:484
  71.3 9.1 %all_to_all.51 = f32[32,1,640]{2,1,0:T(1,128)S(1)} all-to-all(f32[32,1,640]{2,1,0:T(1,128)S(1)} %bitcast.35), channel_id=1, replica_groups=mesh['sec'=4,'grp'=8] {'sec','grp'}, dimensions={0} | all-to-all | bytes 163840 | tf_op jit(solution)/shard_map/all_to_all | solution.py:527
  80.4 0.9 pixels.7
  81.3 9.1 %all_to_all.52 = f32[32,1,640]{2,1,0:T(1,128)S(1)} all-to-all(f32[32,1,640]{2,1,0:T(1,128)S(1)} %bitcast.30), channel_id=1, replica_groups=mesh['sec'=4,'grp'=8] {'sec','grp'}, dimensions={0} | all-to-all | bytes 163840 | tf_op jit(solution)/shard_map/all_to_all | solution.py:527
  90.4 0.0 copy-done.5
  90.4 0.7 last.1
  91.1 8.8 %all_to_all.53 = f32[32,1,128]{2,1,0:T(1,128)S(1)} all-to-all(f32[32,1,128]{2,1,0:T(1,128)S(1)} %bitcast.39), channel_id=1, replica_groups=mesh['sec'=4,'grp'=8] {'sec','grp'}, dimensions={0} | all-to-all | bytes 32768 | tf_op jit(solution)/shard_map/all_to_all | solution.py:527
  99.9 0.8 end.1
Async XLA Ops:
  0.6 17.8 %copy-start.4 = (f32[2,1536]{1,0:T(2,128)S(1)}, f32[2,1536]{1,0:T(2,128)}, u32[]{:S(2)}) copy-start(f32[2,1536]{1,0:T(2,128)} %prior_ref.15) | copy-start | bytes 36868
  0.6 17.8 %copy-start.3 = (s32[16,2048]{1,0:T(8,128)S(1)}, s32[16,2048]{1,0:T(8,128)}, u32[]{:S(2)}) copy-start(s32[16,2048]{1,0:T(8,128)} %mask_ref.7) | copy-start | bytes 393220
  0.7 17.7 %copy-start.2 = (f32[16,2048]{1,0:T(8,128)S(1)}, f32[16,2048]{1,0:T(8,128)}, u32[]{:S(2)}) copy-start(f32[16,2048]{1,0:T(8,128)} %uu_ref.7) | copy-start | bytes 393220
  0.7 17.7 %copy-start.1 = (f32[16,2048]{1,0:T(8,128)S(1)}, f32[16,2048]{1,0:T(8,128)}, u32[]{:S(2)}) copy-start(f32[16,2048]{1,0:T(8,128)} %qu_ref.7) | copy-start | bytes 393220
  0.7 17.7 %copy-start = (f32[16,2048]{1,0:T(8,128)S(1)}, f32[16,2048]{1,0:T(8,128)}, u32[]{:S(2)}) copy-start(f32[16,2048]{1,0:T(8,128)} %qq_ref.7) | copy-start | bytes 393220
  60.5 29.9 %copy-start.5 = (f32[2,4,4,1536]{3,2,1,0:T(4,128)S(1)}, f32[2,4,4,1536]{3,2,1,0:T(4,128)}, u32[]{:S(2)}) copy-start(f32[2,4,4,1536]{3,2,1,0:T(4,128)} %solution_ref.1) | copy-start | bytes 589828

commit v5 on v4

--- a/solution.py
+++ b/solution.py
@@ -106,6 +106,15 @@
     )
 
 
+def spread(two):
+    return by_lane(two, (1, LANES))
+
+
+def unspread(vector):
+    spot = lane_index(vector.shape)
+    return [jnp.sum(jnp.where(spot == b * (LANES // 4), vector, 0.0), axis=1, keepdims=True) for b in range(2)]
+
+
 def by_row(two, shape):
     return jnp.where(row_index(shape) < 4, two[0], two[1])
 
@@ -122,6 +131,10 @@
         (((1,), (1,)), ((), ())),
         preferred_element_type=f32,
     )
+
+
+def turned_product(values, turned_ref, m):
+    return jnp.dot(split_rows(values), turned_ref[m], preferred_element_type=f32)
 
 
 def forward_send(prod, send_ref, buffer_ref, m, sections, cycles, slots):
@@ -272,7 +285,7 @@
         r = jnp.concatenate([residual_ref[0, m], residual_ref[1, m]], axis=0)
         r_ref[m] = r
         square = r * r if square is None else square + r * r
-    send_scalars(send_ref, row_totals(square), slots)
+    send_scalars(send_ref, spread(pair(row_totals(square))), slots)
     for block in blocks:
         block.wait()
     for m in range(slots):
@@ -296,9 +309,15 @@
     d_ref,
     *refs,
 ):
-    if not first:
+    if first:
+        legendre_ref, *refs = refs
+    else:
         r_ref, field_ref, rr_ref, *refs = refs
     send_ref, rr_out, *refs = refs
+    if first:
+        turned_ref, *refs = refs
+        for m in range(legendre_ref.shape[0]):
+            turned_ref[m] = legendre_ref[m].T
     if not first:
         d_out, *refs = refs
     if not last:
@@ -311,9 +330,9 @@
     scalars = received_scalars(recv_ref, slots)
     rr_out[...] = scalars
     if not first:
-        now, before = pair(scalars), pair(rr_ref[...])
-        ratio = tuple(a / b for a, b in zip(now, before))
-        field = field + by_lane(ratio, field.shape) * field_ref[...]
+        lane_ratio = scalars / rr_ref[...]
+        ratio = unspread(lane_ratio)
+        field = field + lane_ratio * field_ref[...]
     if not last:
         field_out[...] = field
     half = LANES // 2
@@ -391,12 +410,12 @@
 
 def step_size(recv_ref, rr_ref, slots):
     curve = pair(received_scalars(recv_ref, slots))
-    two = tuple(a / b for a, b in zip(pair(rr_ref[...]), curve))
+    two = tuple(a / b for a, b in zip(unspread(rr_ref[...]), curve))
     return by_row(two, (ROWS, LANES))[:, :1]
 
 
 def update_kernel(
-    sections, cycles, first, recv_ref, rr_ref, prior_ref, legendre_ref, r_ref, d_ref, *refs
+    sections, cycles, first, recv_ref, rr_ref, prior_ref, legendre_ref, r_ref, d_ref, turned_ref, *refs
 ):
     if not first:
         x_ref, *refs = refs
@@ -410,9 +429,9 @@
         r = next_residual(terms[m], legendre_ref, r_ref, d_ref, m, alpha, prior)
         r_out[m] = r
         square = r * r if square is None else square + r * r
-        forward_send(forward_product(r, legendre_ref, m), send_ref, buffer_ref, m, sections, cycles, slots)
+        forward_send(turned_product(r, turned_ref, m), send_ref, buffer_ref, m, sections, cycles, slots)
         x_out[m] = alpha * d_ref[m] if first else x_ref[m] + alpha * d_ref[m]
-    send_scalars(send_ref, row_totals(square), slots)
+    send_scalars(send_ref, spread(pair(row_totals(square))), slots)
 
 
 def last_kernel(
@@ -459,7 +478,8 @@
     ]
     copies[0].start()
     copies[1].start()
-    now, before = pair(received_scalars(recv_ref, 0)), pair(rr_ref[...])
+    before = unspread(rr_ref[...])
+    now = pair(received_scalars(recv_ref, 0))
     ratios = [now[b] / before[b] for b in range(2)]
 
     def fill(m, carry):
@@ -528,6 +548,7 @@
 
     table = ((4 * total_m, count), bf16)
     blocks = ((slots, 2 * cycles, length), bf16)
+    turned_blocks = ((slots, length, 2 * cycles), bf16)
     send, trig, cosine, sine, rows, r, d = call(
         functools.partial(start_kernel, sections, cycles),
         [message, table, field_like, field_like, blocks, inner, inner],
@@ -548,19 +569,21 @@
     for step in range(ITERS):
         first, last = step == 0, step == ITERS - 1
         recv = exchange(send)
-        carried = () if first else (r, field, rr)
+        carried = (rows,) if first else (r, field, rr)
         out = call(
             functools.partial(pixel_kernel, sections, chunk, first, last),
-            [message, vector] + ([] if first else [inner]) + ([] if last else [field_like]),
+            [message, vector] + [turned_blocks if first else inner] + ([] if last else [field_like]),
             "pixels",
         )(recv, trig, cosine, sine, *noise, inverse_prior, d, *carried)
         send, rr, *out = out
-        if not first:
+        if first:
+            turned, *out = out
+        else:
             d, *out = out
         if not last:
             (field,) = out
         recv = exchange(send)
-        carried = (recv, rr, inverse_prior, rows, r, d) + (() if first else (x,))
+        carried = (recv, rr, inverse_prior, rows, r, d) + (() if last else (turned,)) + (() if first else (x,))
         if last:
             send, residual, solution = call(
                 functools.partial(last_kernel, sections, cycles),

time: 101 us -> 100 us (0.990)
  no operation moved by 1% of the time
where the time goes in v5:
time: 100 us; the launch traced here: 99.9 us
  blocking collectives  87.1 us (87%)
  Pallas kernels  12.1 us (12%)
    all_to_all x9, blocking collectives, exchange(): lax.all_to_all(blocks, ('sec', 'grp'), 0, 0, tiled=True).reshape(x.shape)  87.1 us
    pallas_call x10, Pallas kernels, run(): pl.pallas_call(kernel, out_shape=[jax.ShapeDtypeStruct(shape, dtype) for...  12.1 us

profile of v5, /device:TPU:0, one launch (start us, length us, event | category | flops | bytes accessed | tf_op | source)
XLA Modules:
  0.0 99.9 jit_solution(17307777393027146401)
XLA Ops:
  0.6 0.0 copy-start.4
  0.6 0.0 copy-start.3
  0.7 0.0 copy-start.2
  0.7 0.0 copy-start.1
  0.7 0.0 copy-start
  0.7 3.2 %start.1 = (f32[160,128]{1,0:T(8,128)S(1)}, bf16[128,2048]{1,0:T(8,128)(2,1)S(1)}, f32[32,128]{1,0:T(8,128)S(1)}, f32[32,128]{1,0:T(8,128)S(1)}, bf16[4,256,1536...) custom-call(s32[32]{0:T(128)} %m_hbm.1, f32[1,128]{1,0:T(1,128)} %bitcast.41, ...), custom_call_target="tpu_custom_call" | custom-call | tf_op jit(solution)/shard_map/start/pallas_call | solution.py:504
  3.9 14.5 %all_to_all.45 = f32[32,1,640]{2,1,0:T(1,128)S(1)} all-to-all(f32[32,1,640]{2,1,0:T(1,128)S(1)} %bitcast.33), channel_id=1, replica_groups=mesh['sec'=4,'grp'=8] {'sec','grp'}, dimensions={0} | all-to-all | bytes 163840 | tf_op jit(solution)/shard_map/all_to_all | solution.py:547
  18.5 0.0 copy-done.4
  18.5 0.0 copy-done.3
  18.5 0.0 copy-done.2
  18.5 0.0 copy-done.1
  18.5 0.0 copy-done
  18.5 1.2 %pixels.4 = (f32[160,128]{1,0:T(8,128)S(1)}, f32[1,128]{1,0:T(1,128)S(1)}, bf16[4,1536,256]{2,1,0:T(8,128)(2,1)S(1)}, f32[32,128]{1,0:T(8,128)S(1)}) custom-call(f32[160,128]{1,0:T(8,128)S(1)} %bitcast.29, bf16[128,2048]{1,0:T(8,128)(2,1)S(1)} %get-tuple-element.41.table_ref, f32[32,128]{1,0:T(8,128)S(1)} %get-tuple-element.42.cos_ref, ...), custom_call_target="tpu_custom_call" | custom-call | tf_op jit(solution)/shard_map/pixels/pallas_call | solution.py:504
  19.7 9.1 %all_to_all.46 = f32[32,1,640]{2,1,0:T(1,128)S(1)} all-to-all(f32[32,1,640]{2,1,0:T(1,128)S(1)} %bitcast.36), channel_id=1, replica_groups=mesh['sec'=4,'grp'=8] {'sec','grp'}, dimensions={0} | all-to-all | bytes 163840 | tf_op jit(solution)/shard_map/all_to_all | solution.py:547
  28.8 1.2 %update.3 = (f32[160,128]{1,0:T(8,128)S(1)}, f32[4,8,1536]{2,1,0:T(8,128)S(1)}, f32[4,8,1536]{2,1,0:T(8,128)S(1)}) custom-call(f32[160,128]{1,0:T(8,128)S(1)} %bitcast.28, f32[1,128]{1,0:T(1,128)S(1)} %get-tuple-element.47.rr_ref.refs_2_, f32[2,1536]{1,0:T(2,128)S(1)} %copy-done.4, bf16[4,256,1536]{2,1,0:T(8,128)(2,1)S(1)} %get-tuple-element.45.refs_0_.legendre_ref, ...), custom_call_target="tpu_custom_call" | custom-call | tf_op jit(solution)/shard_map/update/pallas_call | solution.py:504
  30.0 9.1 %all_to_all.47 = f32[32,1,640]{2,1,0:T(1,128)S(1)} all-to-all(f32[32,1,640]{2,1,0:T(1,128)S(1)} %bitcast.37), channel_id=1, replica_groups=mesh['sec'=4,'grp'=8] {'sec','grp'}, dimensions={0} | all-to-all | bytes 163840 | tf_op jit(solution)/shard_map/all_to_all | solution.py:547
  39.2 0.8 pixels.5
  40.0 9.1 %all_to_all.48 = f32[32,1,640]{2,1,0:T(1,128)S(1)} all-to-all(f32[32,1,640]{2,1,0:T(1,128)S(1)} %bitcast.31), channel_id=1, replica_groups=mesh['sec'=4,'grp'=8] {'sec','grp'}, dimensions={0} | all-to-all | bytes 163840 | tf_op jit(solution)/shard_map/all_to_all | solution.py:547
  49.1 1.2 %update.4 = (f32[160,128]{1,0:T(8,128)S(1)}, f32[4,8,1536]{2,1,0:T(8,128)S(1)}, f32[4,8,1536]{2,1,0:T(8,128)S(1)}) custom-call(f32[160,128]{1,0:T(8,128)S(1)} %bitcast.27, f32[1,128]{1,0:T(1,128)S(1)} %get-tuple-element.54.rr_ref.refs_2_, f32[2,1536]{1,0:T(2,128)S(1)} %copy-done.4, bf16[4,256,1536]{2,1,0:T(8,128)(2,1)S(1)} %get-tuple-element.45.refs_0_.legendre_ref, ...), custom_call_target="tpu_custom_call" | custom-call | tf_op jit(solution)/shard_map/update/pallas_call | solution.py:504
  50.3 9.1 %all_to_all.49 = f32[32,1,640]{2,1,0:T(1,128)S(1)} all-to-all(f32[32,1,640]{2,1,0:T(1,128)S(1)} %bitcast.35), channel_id=1, replica_groups=mesh['sec'=4,'grp'=8] {'sec','grp'}, dimensions={0} | all-to-all | bytes 163840 | tf_op jit(solution)/shard_map/all_to_all | solution.py:547
  59.4 0.8 pixels.6
  60.2 9.1 %all_to_all.50 = f32[32,1,640]{2,1,0:T(1,128)S(1)} all-to-all(f32[32,1,640]{2,1,0:T(1,128)S(1)} %bitcast.32), channel_id=1, replica_groups=mesh['sec'=4,'grp'=8] {'sec','grp'}, dimensions={0} | all-to-all | bytes 163840 | tf_op jit(solution)/shard_map/all_to_all | solution.py:547
  69.3 0.0 copy-start.5
  69.3 1.2 %update.5 = (f32[160,128]{1,0:T(8,128)S(1)}, f32[4,8,1536]{2,1,0:T(8,128)S(1)}, f32[4,8,1536]{2,1,0:T(8,128)S(1)}) custom-call(f32[160,128]{1,0:T(8,128)S(1)} %bitcast.26, f32[1,128]{1,0:T(1,128)S(1)} %get-tuple-element.61.rr_ref.refs_2_, f32[2,1536]{1,0:T(2,128)S(1)} %copy-done.4, bf16[4,256,1536]{2,1,0:T(8,128)(2,1)S(1)} %get-tuple-element.45.refs_0_.legendre_ref, ...), custom_call_target="tpu_custom_call" | custom-call | tf_op jit(solution)/shard_map/update/pallas_call | solution.py:504
  70.5 9.1 %all_to_all.51 = f32[32,1,640]{2,1,0:T(1,128)S(1)} all-to-all(f32[32,1,640]{2,1,0:T(1,128)S(1)} %bitcast.34), channel_id=1, replica_groups=mesh['sec'=4,'grp'=8] {'sec','grp'}, dimensions={0} | all-to-all | bytes 163840 | tf_op jit(solution)/shard_map/all_to_all | solution.py:547
  79.7 0.8 pixels.7
  80.5 9.1 %all_to_all.52 = f32[32,1,640]{2,1,0:T(1,128)S(1)} all-to-all(f32[32,1,640]{2,1,0:T(1,128)S(1)} %bitcast.30), channel_id=1, replica_groups=mesh['sec'=4,'grp'=8] {'sec','grp'}, dimensions={0} | all-to-all | bytes 163840 | tf_op jit(solution)/shard_map/all_to_all | solution.py:547
  89.6 0.0 copy-done.5
  89.6 0.7 last.1
  90.3 8.8 %all_to_all.53 = f32[32,1,128]{2,1,0:T(1,128)S(1)} all-to-all(f32[32,1,128]{2,1,0:T(1,128)S(1)} %bitcast.39), channel_id=1, replica_groups=mesh['sec'=4,'grp'=8] {'sec','grp'}, dimensions={0} | all-to-all | bytes 32768 | tf_op jit(solution)/shard_map/all_to_all | solution.py:547
  99.1 0.8 end.1
Async XLA Ops:
  0.6 17.8 %copy-start.4 = (f32[2,1536]{1,0:T(2,128)S(1)}, f32[2,1536]{1,0:T(2,128)}, u32[]{:S(2)}) copy-start(f32[2,1536]{1,0:T(2,128)} %prior_ref.15) | copy-start | bytes 36868
  0.6 17.8 %copy-start.3 = (s32[16,2048]{1,0:T(8,128)S(1)}, s32[16,2048]{1,0:T(8,128)}, u32[]{:S(2)}) copy-start(s32[16,2048]{1,0:T(8,128)} %mask_ref.7) | copy-start | bytes 393220
  0.7 17.8 %copy-start.2 = (f32[16,2048]{1,0:T(8,128)S(1)}, f32[16,2048]{1,0:T(8,128)}, u32[]{:S(2)}) copy-start(f32[16,2048]{1,0:T(8,128)} %uu_ref.7) | copy-start | bytes 393220
  0.7 17.8 %copy-start.1 = (f32[16,2048]{1,0:T(8,128)S(1)}, f32[16,2048]{1,0:T(8,128)}, u32[]{:S(2)}) copy-start(f32[16,2048]{1,0:T(8,128)} %qu_ref.7) | copy-start | bytes 393220
  0.7 17.8 %copy-start = (f32[16,2048]{1,0:T(8,128)S(1)}, f32[16,2048]{1,0:T(8,128)}, u32[]{:S(2)}) copy-start(f32[16,2048]{1,0:T(8,128)} %qq_ref.7) | copy-start | bytes 393220
  69.3 20.3 %copy-start.5 = (f32[2,4,4,1536]{3,2,1,0:T(4,128)S(1)}, f32[2,4,4,1536]{3,2,1,0:T(4,128)}, u32[]{:S(2)}) copy-start(f32[2,4,4,1536]{3,2,1,0:T(4,128)} %solution_ref.1) | copy-start | bytes 589828

commit v6 on v5

--- a/solution.py
+++ b/solution.py
@@ -316,8 +316,6 @@
     send_ref, rr_out, *refs = refs
     if first:
         turned_ref, *refs = refs
-        for m in range(legendre_ref.shape[0]):
-            turned_ref[m] = legendre_ref[m].T
     if not first:
         d_out, *refs = refs
     if not last:
@@ -382,6 +380,9 @@
         product = prior * d * d
         own = product if own is None else own + product
 
+    if first:
+        for m in range(slots):
+            turned_ref[m] = legendre_ref[m].T
     send_scalars(send_ref, curve + row_totals(own), slots)
 
 
@@ -425,12 +426,16 @@
     prior = prior_rows(prior_ref)
     square = None
     terms = [image_terms(recv_ref, buffer_ref, m, sections, cycles, slots) for m in range(slots)]
-    for m in range(slots):
-        r = next_residual(terms[m], legendre_ref, r_ref, d_ref, m, alpha, prior)
-        r_out[m] = r
-        square = r * r if square is None else square + r * r
-        forward_send(turned_product(r, turned_ref, m), send_ref, buffer_ref, m, sections, cycles, slots)
-        x_out[m] = alpha * d_ref[m] if first else x_ref[m] + alpha * d_ref[m]
+    waiting = None
+    for m in range(slots + 1):
+        if m < slots:
+            r = next_residual(terms[m], legendre_ref, r_ref, d_ref, m, alpha, prior)
+            r_out[m] = r
+            square = r * r if square is None else square + r * r
+            x_out[m] = alpha * d_ref[m] if first else x_ref[m] + alpha * d_ref[m]
+        if waiting is not None:
+            forward_send(turned_product(waiting, turned_ref, m - 1), send_ref, buffer_ref, m - 1, sections, cycles, slots)
+        waiting = r
     send_scalars(send_ref, spread(pair(row_totals(square))), slots)
 
 

time: 100 us -> 99.9 us (level)
  no operation moved by 1% of the time
where the time goes in v6:
time: 99.9 us; the launch traced here: 99.6 us
  blocking collectives  87.1 us (87%)
  Pallas kernels  11.7 us (12%)
    all_to_all x9, blocking collectives, exchange(): lax.all_to_all(blocks, ('sec', 'grp'), 0, 0, tiled=True).reshape(x.shape)  87.1 us
    pallas_call x10, Pallas kernels, run(): pl.pallas_call(kernel, out_shape=[jax.ShapeDtypeStruct(shape, dtype) for...  11.7 us

profile of v6, /device:TPU:0, one launch (start us, length us, event | category | flops | bytes accessed | tf_op | source)
XLA Modules:
  0.0 99.6 jit_solution(15287460363404668085)
XLA Ops:
  0.6 0.0 copy-start.4
  0.6 0.0 copy-start.3
  0.7 0.0 copy-start.2
  0.7 0.0 copy-start.1
  0.7 0.0 copy-start
  0.7 3.2 %start.1 = (f32[160,128]{1,0:T(8,128)S(1)}, bf16[128,2048]{1,0:T(8,128)(2,1)S(1)}, f32[32,128]{1,0:T(8,128)S(1)}, f32[32,128]{1,0:T(8,128)S(1)}, bf16[4,256,1536...) custom-call(s32[32]{0:T(128)} %m_hbm.1, f32[1,128]{1,0:T(1,128)} %bitcast.41, ...), custom_call_target="tpu_custom_call" | custom-call | tf_op jit(solution)/shard_map/start/pallas_call | solution.py:509
  3.9 14.5 %all_to_all.45 = f32[32,1,640]{2,1,0:T(1,128)S(1)} all-to-all(f32[32,1,640]{2,1,0:T(1,128)S(1)} %bitcast.33), channel_id=1, replica_groups=mesh['sec'=4,'grp'=8] {'sec','grp'}, dimensions={0} | all-to-all | bytes 163840 | tf_op jit(solution)/shard_map/all_to_all | solution.py:552
  18.5 0.0 copy-done.4
  18.5 0.0 copy-done.3
  18.5 0.0 copy-done.2
  18.5 0.0 copy-done.1
  18.5 0.0 copy-done
  18.5 1.2 %pixels.4 = (f32[160,128]{1,0:T(8,128)S(1)}, f32[1,128]{1,0:T(1,128)S(1)}, bf16[4,1536,256]{2,1,0:T(8,128)(2,1)S(1)}, f32[32,128]{1,0:T(8,128)S(1)}) custom-call(f32[160,128]{1,0:T(8,128)S(1)} %bitcast.29, bf16[128,2048]{1,0:T(8,128)(2,1)S(1)} %get-tuple-element.41.table_ref, f32[32,128]{1,0:T(8,128)S(1)} %get-tuple-element.42.cos_ref, ...), custom_call_target="tpu_custom_call" | custom-call | tf_op jit(solution)/shard_map/pixels/pallas_call | solution.py:509
  19.7 9.1 %all_to_all.46 = f32[32,1,640]{2,1,0:T(1,128)S(1)} all-to-all(f32[32,1,640]{2,1,0:T(1,128)S(1)} %bitcast.36), channel_id=1, replica_groups=mesh['sec'=4,'grp'=8] {'sec','grp'}, dimensions={0} | all-to-all | bytes 163840 | tf_op jit(solution)/shard_map/all_to_all | solution.py:552
  28.8 1.1 %update.3 = (f32[160,128]{1,0:T(8,128)S(1)}, f32[4,8,1536]{2,1,0:T(8,128)S(1)}, f32[4,8,1536]{2,1,0:T(8,128)S(1)}) custom-call(f32[160,128]{1,0:T(8,128)S(1)} %bitcast.28, f32[1,128]{1,0:T(1,128)S(1)} %get-tuple-element.47.rr_ref.refs_2_, f32[2,1536]{1,0:T(2,128)S(1)} %copy-done.4, bf16[4,256,1536]{2,1,0:T(8,128)(2,1)S(1)} %get-tuple-element.45.refs_0_.legendre_ref, ...), custom_call_target="tpu_custom_call" | custom-call | tf_op jit(solution)/shard_map/update/pallas_call | solution.py:509
  29.9 9.1 %all_to_all.47 = f32[32,1,640]{2,1,0:T(1,128)S(1)} all-to-all(f32[32,1,640]{2,1,0:T(1,128)S(1)} %bitcast.37), channel_id=1, replica_groups=mesh['sec'=4,'grp'=8] {'sec','grp'}, dimensions={0} | all-to-all | bytes 163840 | tf_op jit(solution)/shard_map/all_to_all | solution.py:552
  39.0 0.8 pixels.5
  39.8 9.1 %all_to_all.48 = f32[32,1,640]{2,1,0:T(1,128)S(1)} all-to-all(f32[32,1,640]{2,1,0:T(1,128)S(1)} %bitcast.31), channel_id=1, replica_groups=mesh['sec'=4,'grp'=8] {'sec','grp'}, dimensions={0} | all-to-all | bytes 163840 | tf_op jit(solution)/shard_map/all_to_all | solution.py:552
  48.9 1.1 %update.4 = (f32[160,128]{1,0:T(8,128)S(1)}, f32[4,8,1536]{2,1,0:T(8,128)S(1)}, f32[4,8,1536]{2,1,0:T(8,128)S(1)}) custom-call(f32[160,128]{1,0:T(8,128)S(1)} %bitcast.27, f32[1,128]{1,0:T(1,128)S(1)} %get-tuple-element.54.rr_ref.refs_2_, f32[2,1536]{1,0:T(2,128)S(1)} %copy-done.4, bf16[4,256,1536]{2,1,0:T(8,128)(2,1)S(1)} %get-tuple-element.45.refs_0_.legendre_ref, ...), custom_call_target="tpu_custom_call" | custom-call | tf_op jit(solution)/shard_map/update/pallas_call | solution.py:509
  50.0 9.1 %all_to_all.49 = f32[32,1,640]{2,1,0:T(1,128)S(1)} all-to-all(f32[32,1,640]{2,1,0:T(1,128)S(1)} %bitcast.35), channel_id=1, replica_groups=mesh['sec'=4,'grp'=8] {'sec','grp'}, dimensions={0} | all-to-all | bytes 163840 | tf_op jit(solution)/shard_map/all_to_all | solution.py:552
  59.1 0.8 pixels.6
  60.0 9.1 %all_to_all.50 = f32[32,1,640]{2,1,0:T(1,128)S(1)} all-to-all(f32[32,1,640]{2,1,0:T(1,128)S(1)} %bitcast.32), channel_id=1, replica_groups=mesh['sec'=4,'grp'=8] {'sec','grp'}, dimensions={0} | all-to-all | bytes 163840 | tf_op jit(solution)/shard_map/all_to_all | solution.py:552
  69.1 0.0 copy-start.5
  69.1 1.1 %update.5 = (f32[160,128]{1,0:T(8,128)S(1)}, f32[4,8,1536]{2,1,0:T(8,128)S(1)}, f32[4,8,1536]{2,1,0:T(8,128)S(1)}) custom-call(f32[160,128]{1,0:T(8,128)S(1)} %bitcast.26, f32[1,128]{1,0:T(1,128)S(1)} %get-tuple-element.61.rr_ref.refs_2_, f32[2,1536]{1,0:T(2,128)S(1)} %copy-done.4, bf16[4,256,1536]{2,1,0:T(8,128)(2,1)S(1)} %get-tuple-element.45.refs_0_.legendre_ref, ...), custom_call_target="tpu_custom_call" | custom-call | tf_op jit(solution)/shard_map/update/pallas_call | solution.py:509
  70.2 9.1 %all_to_all.51 = f32[32,1,640]{2,1,0:T(1,128)S(1)} all-to-all(f32[32,1,640]{2,1,0:T(1,128)S(1)} %bitcast.34), channel_id=1, replica_groups=mesh['sec'=4,'grp'=8] {'sec','grp'}, dimensions={0} | all-to-all | bytes 163840 | tf_op jit(solution)/shard_map/all_to_all | solution.py:552
  79.3 0.8 pixels.7
  80.1 9.1 %all_to_all.52 = f32[32,1,640]{2,1,0:T(1,128)S(1)} all-to-all(f32[32,1,640]{2,1,0:T(1,128)S(1)} %bitcast.30), channel_id=1, replica_groups=mesh['sec'=4,'grp'=8] {'sec','grp'}, dimensions={0} | all-to-all | bytes 163840 | tf_op jit(solution)/shard_map/all_to_all | solution.py:552
  89.2 0.0 copy-done.5
  89.2 0.7 last.1
  89.9 8.8 %all_to_all.53 = f32[32,1,128]{2,1,0:T(1,128)S(1)} all-to-all(f32[32,1,128]{2,1,0:T(1,128)S(1)} %bitcast.39), channel_id=1, replica_groups=mesh['sec'=4,'grp'=8] {'sec','grp'}, dimensions={0} | all-to-all | bytes 32768 | tf_op jit(solution)/shard_map/all_to_all | solution.py:552
  98.7 0.8 end.1
Async XLA Ops:
  0.6 17.8 %copy-start.4 = (f32[2,1536]{1,0:T(2,128)S(1)}, f32[2,1536]{1,0:T(2,128)}, u32[]{:S(2)}) copy-start(f32[2,1536]{1,0:T(2,128)} %prior_ref.15) | copy-start | bytes 36868
  0.6 17.8 %copy-start.3 = (s32[16,2048]{1,0:T(8,128)S(1)}, s32[16,2048]{1,0:T(8,128)}, u32[]{:S(2)}) copy-start(s32[16,2048]{1,0:T(8,128)} %mask_ref.7) | copy-start | bytes 393220
  0.7 17.8 %copy-start.2 = (f32[16,2048]{1,0:T(8,128)S(1)}, f32[16,2048]{1,0:T(8,128)}, u32[]{:S(2)}) copy-start(f32[16,2048]{1,0:T(8,128)} %uu_ref.7) | copy-start | bytes 393220
  0.7 17.8 %copy-start.1 = (f32[16,2048]{1,0:T(8,128)S(1)}, f32[16,2048]{1,0:T(8,128)}, u32[]{:S(2)}) copy-start(f32[16,2048]{1,0:T(8,128)} %qu_ref.7) | copy-start | bytes 393220
  0.7 17.8 %copy-start = (f32[16,2048]{1,0:T(8,128)S(1)}, f32[16,2048]{1,0:T(8,128)}, u32[]{:S(2)}) copy-start(f32[16,2048]{1,0:T(8,128)} %qq_ref.7) | copy-start | bytes 393220
  69.1 20.2 %copy-start.5 = (f32[2,4,4,1536]{3,2,1,0:T(4,128)S(1)}, f32[2,4,4,1536]{3,2,1,0:T(4,128)}, u32[]{:S(2)}) copy-start(f32[2,4,4,1536]{3,2,1,0:T(4,128)} %solution_ref.1) | copy-start | bytes 589828

commit v7 on v6

--- a/solution.py
+++ b/solution.py
@@ -342,7 +342,7 @@
     count = qq_ref.shape[1]
     cycles = qq_ref.shape[0]
     top = 2 * total_m
-    folded = None
+    pieces = []
     for c in range(count // chunk):
         here = slice(c * chunk, (c + 1) * chunk)
         pixels = lax.dot_general(
@@ -355,11 +355,11 @@
             q = pixels[2 * b * cycles : (2 * b + 1) * cycles]
             u = pixels[(2 * b + 1) * cycles : (2 * b + 2) * cycles]
             parts += [nqq * q + nqu * u, nqu * q + nuu * u]
-        weighted = jnp.concatenate(parts, axis=0).astype(bf16)
-        part = lax.dot_general(
-            table_ref[:top, here], weighted, (((1,), (1,)), ((), ())), preferred_element_type=f32
-        )
-        folded = part if folded is None else folded + part
+        pieces.append(jnp.concatenate(parts, axis=0).astype(bf16))
+    weighted = jnp.concatenate(pieces, axis=1)
+    folded = lax.dot_general(
+        table_ref[:top, :], weighted, (((1,), (1,)), ((), ())), preferred_element_type=f32
+    )
     folded = jnp.concatenate([folded[:total_m], folded[total_m:]], axis=1)
     out = folded * cosine - pltpu.roll(folded, half, 1) * sine
     curve = jnp.sum(field * out, axis=0, keepdims=True)

time: 99.9 us -> 99.8 us (level)
  no operation moved by 1% of the time
where the time goes in v7:
time: 99.8 us; the launch traced here: 99.5 us
  blocking collectives  87.1 us (87%)
  Pallas kernels  11.6 us (12%)
    all_to_all x9, blocking collectives, exchange(): lax.all_to_all(blocks, ('sec', 'grp'), 0, 0, tiled=True).reshape(x.shape)  87.1 us
    pallas_call x10, Pallas kernels, run(): pl.pallas_call(kernel, out_shape=[jax.ShapeDtypeStruct(shape, dtype) for...  11.6 us

profile of v7, /device:TPU:0, one launch (start us, length us, event | category | flops | bytes accessed | tf_op | source)
XLA Modules:
  0.0 99.5 jit_solution(12341103541387167442)
XLA Ops:
  0.6 0.0 copy-start.4
  0.6 0.0 copy-start.3
  0.7 0.0 copy-start.2
  0.7 0.0 copy-start.1
  0.7 0.0 copy-start
  0.7 3.2 %start.1 = (f32[160,128]{1,0:T(8,128)S(1)}, bf16[128,2048]{1,0:T(8,128)(2,1)S(1)}, f32[32,128]{1,0:T(8,128)S(1)}, f32[32,128]{1,0:T(8,128)S(1)}, bf16[4,256,1536...) custom-call(s32[32]{0:T(128)} %m_hbm.1, f32[1,128]{1,0:T(1,128)} %bitcast.41, ...), custom_call_target="tpu_custom_call" | custom-call | tf_op jit(solution)/shard_map/start/pallas_call | solution.py:509
  3.9 14.5 %all_to_all.45 = f32[32,1,640]{2,1,0:T(1,128)S(1)} all-to-all(f32[32,1,640]{2,1,0:T(1,128)S(1)} %bitcast.33), channel_id=1, replica_groups=mesh['sec'=4,'grp'=8] {'sec','grp'}, dimensions={0} | all-to-all | bytes 163840 | tf_op jit(solution)/shard_map/all_to_all | solution.py:552
  18.5 0.0 copy-done.4
  18.5 0.0 copy-done.3
  18.5 0.0 copy-done.2
  18.5 0.0 copy-done.1
  18.5 0.0 copy-done
  18.5 1.2 %pixels.4 = (f32[160,128]{1,0:T(8,128)S(1)}, f32[1,128]{1,0:T(1,128)S(1)}, bf16[4,1536,256]{2,1,0:T(8,128)(2,1)S(1)}, f32[32,128]{1,0:T(8,128)S(1)}) custom-call(f32[160,128]{1,0:T(8,128)S(1)} %bitcast.29, bf16[128,2048]{1,0:T(8,128)(2,1)S(1)} %get-tuple-element.41.table_ref, f32[32,128]{1,0:T(8,128)S(1)} %get-tuple-element.42.cos_ref, ...), custom_call_target="tpu_custom_call" | custom-call | tf_op jit(solution)/shard_map/pixels/pallas_call | solution.py:509
  19.7 9.1 %all_to_all.46 = f32[32,1,640]{2,1,0:T(1,128)S(1)} all-to-all(f32[32,1,640]{2,1,0:T(1,128)S(1)} %bitcast.36), channel_id=1, replica_groups=mesh['sec'=4,'grp'=8] {'sec','grp'}, dimensions={0} | all-to-all | bytes 163840 | tf_op jit(solution)/shard_map/all_to_all | solution.py:552
  28.8 1.1 %update.3 = (f32[160,128]{1,0:T(8,128)S(1)}, f32[4,8,1536]{2,1,0:T(8,128)S(1)}, f32[4,8,1536]{2,1,0:T(8,128)S(1)}) custom-call(f32[160,128]{1,0:T(8,128)S(1)} %bitcast.28, f32[1,128]{1,0:T(1,128)S(1)} %get-tuple-element.47.rr_ref.refs_2_, f32[2,1536]{1,0:T(2,128)S(1)} %copy-done.4, bf16[4,256,1536]{2,1,0:T(8,128)(2,1)S(1)} %get-tuple-element.45.refs_0_.legendre_ref, ...), custom_call_target="tpu_custom_call" | custom-call | tf_op jit(solution)/shard_map/update/pallas_call | solution.py:509
  29.9 9.1 %all_to_all.47 = f32[32,1,640]{2,1,0:T(1,128)S(1)} all-to-all(f32[32,1,640]{2,1,0:T(1,128)S(1)} %bitcast.37), channel_id=1, replica_groups=mesh['sec'=4,'grp'=8] {'sec','grp'}, dimensions={0} | all-to-all | bytes 163840 | tf_op jit(solution)/shard_map/all_to_all | solution.py:552
  39.0 0.8 pixels.5
  39.8 9.1 %all_to_all.48 = f32[32,1,640]{2,1,0:T(1,128)S(1)} all-to-all(f32[32,1,640]{2,1,0:T(1,128)S(1)} %bitcast.31), channel_id=1, replica_groups=mesh['sec'=4,'grp'=8] {'sec','grp'}, dimensions={0} | all-to-all | bytes 163840 | tf_op jit(solution)/shard_map/all_to_all | solution.py:552
  48.9 1.1 %update.4 = (f32[160,128]{1,0:T(8,128)S(1)}, f32[4,8,1536]{2,1,0:T(8,128)S(1)}, f32[4,8,1536]{2,1,0:T(8,128)S(1)}) custom-call(f32[160,128]{1,0:T(8,128)S(1)} %bitcast.27, f32[1,128]{1,0:T(1,128)S(1)} %get-tuple-element.54.rr_ref.refs_2_, f32[2,1536]{1,0:T(2,128)S(1)} %copy-done.4, bf16[4,256,1536]{2,1,0:T(8,128)(2,1)S(1)} %get-tuple-element.45.refs_0_.legendre_ref, ...), custom_call_target="tpu_custom_call" | custom-call | tf_op jit(solution)/shard_map/update/pallas_call | solution.py:509
  50.0 9.1 %all_to_all.49 = f32[32,1,640]{2,1,0:T(1,128)S(1)} all-to-all(f32[32,1,640]{2,1,0:T(1,128)S(1)} %bitcast.35), channel_id=1, replica_groups=mesh['sec'=4,'grp'=8] {'sec','grp'}, dimensions={0} | all-to-all | bytes 163840 | tf_op jit(solution)/shard_map/all_to_all | solution.py:552
  59.1 0.8 pixels.6
  59.9 9.1 %all_to_all.50 = f32[32,1,640]{2,1,0:T(1,128)S(1)} all-to-all(f32[32,1,640]{2,1,0:T(1,128)S(1)} %bitcast.32), channel_id=1, replica_groups=mesh['sec'=4,'grp'=8] {'sec','grp'}, dimensions={0} | all-to-all | bytes 163840 | tf_op jit(solution)/shard_map/all_to_all | solution.py:552
  69.0 0.0 copy-start.5
  69.0 1.1 %update.5 = (f32[160,128]{1,0:T(8,128)S(1)}, f32[4,8,1536]{2,1,0:T(8,128)S(1)}, f32[4,8,1536]{2,1,0:T(8,128)S(1)}) custom-call(f32[160,128]{1,0:T(8,128)S(1)} %bitcast.26, f32[1,128]{1,0:T(1,128)S(1)} %get-tuple-element.61.rr_ref.refs_2_, f32[2,1536]{1,0:T(2,128)S(1)} %copy-done.4, bf16[4,256,1536]{2,1,0:T(8,128)(2,1)S(1)} %get-tuple-element.45.refs_0_.legendre_ref, ...), custom_call_target="tpu_custom_call" | custom-call | tf_op jit(solution)/shard_map/update/pallas_call | solution.py:509
  70.1 9.1 %all_to_all.51 = f32[32,1,640]{2,1,0:T(1,128)S(1)} all-to-all(f32[32,1,640]{2,1,0:T(1,128)S(1)} %bitcast.34), channel_id=1, replica_groups=mesh['sec'=4,'grp'=8] {'sec','grp'}, dimensions={0} | all-to-all | bytes 163840 | tf_op jit(solution)/shard_map/all_to_all | solution.py:552
  79.2 0.8 pixels.7
  80.1 9.1 %all_to_all.52 = f32[32,1,640]{2,1,0:T(1,128)S(1)} all-to-all(f32[32,1,640]{2,1,0:T(1,128)S(1)} %bitcast.30), channel_id=1, replica_groups=mesh['sec'=4,'grp'=8] {'sec','grp'}, dimensions={0} | all-to-all | bytes 163840 | tf_op jit(solution)/shard_map/all_to_all | solution.py:552
  89.2 0.0 copy-done.5
  89.2 0.7 last.1
  89.8 8.8 %all_to_all.53 = f32[32,1,128]{2,1,0:T(1,128)S(1)} all-to-all(f32[32,1,128]{2,1,0:T(1,128)S(1)} %bitcast.39), channel_id=1, replica_groups=mesh['sec'=4,'grp'=8] {'sec','grp'}, dimensions={0} | all-to-all | bytes 32768 | tf_op jit(solution)/shard_map/all_to_all | solution.py:552
  98.7 0.8 end.1
Async XLA Ops:
  0.6 17.8 %copy-start.4 = (f32[2,1536]{1,0:T(2,128)S(1)}, f32[2,1536]{1,0:T(2,128)}, u32[]{:S(2)}) copy-start(f32[2,1536]{1,0:T(2,128)} %prior_ref.15) | copy-start | bytes 36868
  0.6 17.8 %copy-start.3 = (s32[16,2048]{1,0:T(8,128)S(1)}, s32[16,2048]{1,0:T(8,128)}, u32[]{:S(2)}) copy-start(s32[16,2048]{1,0:T(8,128)} %mask_ref.7) | copy-start | bytes 393220
  0.7 17.8 %copy-start.2 = (f32[16,2048]{1,0:T(8,128)S(1)}, f32[16,2048]{1,0:T(8,128)}, u32[]{:S(2)}) copy-start(f32[16,2048]{1,0:T(8,128)} %uu_ref.7) | copy-start | bytes 393220
  0.7 17.8 %copy-start.1 = (f32[16,2048]{1,0:T(8,128)S(1)}, f32[16,2048]{1,0:T(8,128)}, u32[]{:S(2)}) copy-start(f32[16,2048]{1,0:T(8,128)} %qu_ref.7) | copy-start | bytes 393220
  0.7 17.8 %copy-start = (f32[16,2048]{1,0:T(8,128)S(1)}, f32[16,2048]{1,0:T(8,128)}, u32[]{:S(2)}) copy-start(f32[16,2048]{1,0:T(8,128)} %qq_ref.7) | copy-start | bytes 393220
  69.0 20.1 %copy-start.5 = (f32[2,4,4,1536]{3,2,1,0:T(4,128)S(1)}, f32[2,4,4,1536]{3,2,1,0:T(4,128)}, u32[]{:S(2)}) copy-start(f32[2,4,4,1536]{3,2,1,0:T(4,128)} %solution_ref.1) | copy-start | bytes 589828

commit v8 on v7

--- a/solution.py
+++ b/solution.py
@@ -304,18 +304,17 @@
     qq_ref,
     qu_ref,
     uu_ref,
-    mask_ref,
     prior_ref,
     d_ref,
     *refs,
 ):
     if first:
-        legendre_ref, *refs = refs
+        mask_ref, legendre_ref, *refs = refs
     else:
         r_ref, field_ref, rr_ref, *refs = refs
     send_ref, rr_out, *refs = refs
     if first:
-        turned_ref, *refs = refs
+        turned_ref, *refs, nqq_out, nqu_out, nuu_out = refs
     if not first:
         d_out, *refs = refs
     if not last:
@@ -348,8 +347,11 @@
         pixels = lax.dot_general(
             both, table_ref[:, here], (((0,), (0,)), ((), ())), preferred_element_type=f32
         )
-        mask = mask_ref[:, here].astype(f32)
-        nqq, nqu, nuu = mask * qq_ref[:, here], mask * qu_ref[:, here], mask * uu_ref[:, here]
+        nqq, nqu, nuu = qq_ref[:, here], qu_ref[:, here], uu_ref[:, here]
+        if first:
+            mask = mask_ref[:, here].astype(f32)
+            nqq, nqu, nuu = mask * nqq, mask * nqu, mask * nuu
+            nqq_out[:, here], nqu_out[:, here], nuu_out[:, here] = nqq, nqu, nuu
         parts = []
         for b in range(2):
             q = pixels[2 * b * cycles : (2 * b + 1) * cycles]
@@ -570,19 +572,21 @@
             pltpu.SemaphoreType.DMA((slots,)),
         ),
     )(m_values, cycle_phase.reshape(-1, LANES), residual_in, direction_in, legendre.reshape(blocks[0]))
-    noise = (noise_qq, noise_qu, noise_uu, pixel_mask)
+    noise = (noise_qq, noise_qu, noise_uu)
     for step in range(ITERS):
         first, last = step == 0, step == ITERS - 1
         recv = exchange(send)
-        carried = (rows,) if first else (r, field, rr)
+        carried = (pixel_mask, rows) if first else (r, field, rr)
         out = call(
             functools.partial(pixel_kernel, sections, chunk, first, last),
-            [message, vector] + [turned_blocks if first else inner] + ([] if last else [field_like]),
+            [message, vector] + [turned_blocks if first else inner] + ([] if last else [field_like]) + [(noise_qq.shape, f32)] * (3 if first else 0),
             "pixels",
         )(recv, trig, cosine, sine, *noise, inverse_prior, d, *carried)
         send, rr, *out = out
         if first:
             turned, *out = out
+            *out, nqq, nqu, nuu = out
+            noise = (nqq, nqu, nuu)
         else:
             d, *out = out
         if not last:

time: 99.8 us -> 99.8 us (level)
  no operation moved by 1% of the time
where the time goes in v8:
time: 99.8 us; the launch traced here: 99.5 us
  blocking collectives  87.1 us (87%)
  Pallas kernels  11.7 us (12%)
    all_to_all x9, blocking collectives, exchange(): lax.all_to_all(blocks, ('sec', 'grp'), 0, 0, tiled=True).reshape(x.shape)  87.1 us
    pallas_call x10, Pallas kernels, run(): pl.pallas_call(kernel, out_shape=[jax.ShapeDtypeStruct(shape, dtype) for...  11.7 us

profile of v8, /device:TPU:0, one launch (start us, length us, event | category | flops | bytes accessed | tf_op | source)
XLA Modules:
  0.0 99.5 jit_solution(10879925621771909618)
XLA Ops:
  0.6 0.0 copy-start
  0.6 0.0 copy-start.5
  0.7 0.0 copy-start.4
  0.7 0.0 copy-start.3
  0.7 0.0 copy-start.2
  0.7 3.2 %start.1 = (f32[160,128]{1,0:T(8,128)S(1)}, bf16[128,2048]{1,0:T(8,128)(2,1)S(1)}, f32[32,128]{1,0:T(8,128)S(1)}, f32[32,128]{1,0:T(8,128)S(1)}, bf16[4,256,1536...) custom-call(s32[32]{0:T(128)} %m_hbm.1, f32[1,128]{1,0:T(1,128)} %bitcast.41, ...), custom_call_target="tpu_custom_call" | custom-call | tf_op jit(solution)/shard_map/start/pallas_call | solution.py:511
  3.9 14.5 %all_to_all.45 = f32[32,1,640]{2,1,0:T(1,128)S(1)} all-to-all(f32[32,1,640]{2,1,0:T(1,128)S(1)} %bitcast.34), channel_id=1, replica_groups=mesh['sec'=4,'grp'=8] {'sec','grp'}, dimensions={0} | all-to-all | bytes 163840 | tf_op jit(solution)/shard_map/all_to_all | solution.py:554
  18.5 0.0 copy-done
  18.5 0.0 copy-done.5
  18.5 0.0 copy-done.4
  18.5 0.0 copy-done.3
  18.5 0.0 copy-done.2
  18.5 1.2 %pixels.4 = (f32[160,128]{1,0:T(8,128)S(1)}, f32[1,128]{1,0:T(1,128)S(1)}, bf16[4,1536,256]{2,1,0:T(8,128)(2,1)S(1)}, f32[32,128]{1,0:T(8,128)S(1)}, f32[16,2048...) custom-call(f32[160,128]{1,0:T(8,128)S(1)} %bitcast.26, ...), custom_call_target="tpu_custom_call" | custom-call | tf_op jit(solution)/shard_map/pixels/pallas_call | solution.py:511
  19.7 9.1 %all_to_all.46 = f32[32,1,640]{2,1,0:T(1,128)S(1)} all-to-all(f32[32,1,640]{2,1,0:T(1,128)S(1)} %bitcast.31), channel_id=1, replica_groups=mesh['sec'=4,'grp'=8] {'sec','grp'}, dimensions={0} | all-to-all | bytes 163840 | tf_op jit(solution)/shard_map/all_to_all | solution.py:554
  28.8 1.1 %update.3 = (f32[160,128]{1,0:T(8,128)S(1)}, f32[4,8,1536]{2,1,0:T(8,128)S(1)}, f32[4,8,1536]{2,1,0:T(8,128)S(1)}) custom-call(f32[160,128]{1,0:T(8,128)S(1)} %bitcast.29, f32[1,128]{1,0:T(1,128)S(1)} %get-tuple-element.50.rr_ref.refs_2_, f32[2,1536]{1,0:T(2,128)S(1)} %copy-done, bf16[4,256,1536]{2,1,0:T(8,128)(2,1)S(1)} %get-tuple-element.48.refs_1_.legendre_ref, ...), custom_call_target="tpu_custom_call" | custom-call | tf_op jit(solution)/shard_map/update/pallas_call | solution.py:511
  29.9 9.1 %all_to_all.47 = f32[32,1,640]{2,1,0:T(1,128)S(1)} all-to-all(f32[32,1,640]{2,1,0:T(1,128)S(1)} %bitcast.37), channel_id=1, replica_groups=mesh['sec'=4,'grp'=8] {'sec','grp'}, dimensions={0} | all-to-all | bytes 163840 | tf_op jit(solution)/shard_map/all_to_all | solution.py:554
  39.0 0.8 pixels.5
  39.8 9.1 %all_to_all.48 = f32[32,1,640]{2,1,0:T(1,128)S(1)} all-to-all(f32[32,1,640]{2,1,0:T(1,128)S(1)} %bitcast.32), channel_id=1, replica_groups=mesh['sec'=4,'grp'=8] {'sec','grp'}, dimensions={0} | all-to-all | bytes 163840 | tf_op jit(solution)/shard_map/all_to_all | solution.py:554
  48.9 1.1 %update.4 = (f32[160,128]{1,0:T(8,128)S(1)}, f32[4,8,1536]{2,1,0:T(8,128)S(1)}, f32[4,8,1536]{2,1,0:T(8,128)S(1)}) custom-call(f32[160,128]{1,0:T(8,128)S(1)} %bitcast.28, f32[1,128]{1,0:T(1,128)S(1)} %get-tuple-element.60.rr_ref.refs_2_, f32[2,1536]{1,0:T(2,128)S(1)} %copy-done, bf16[4,256,1536]{2,1,0:T(8,128)(2,1)S(1)} %get-tuple-element.48.refs_1_.legendre_ref, ...), custom_call_target="tpu_custom_call" | custom-call | tf_op jit(solution)/shard_map/update/pallas_call | solution.py:511
  50.0 9.1 %all_to_all.49 = f32[32,1,640]{2,1,0:T(1,128)S(1)} all-to-all(f32[32,1,640]{2,1,0:T(1,128)S(1)} %bitcast.36), channel_id=1, replica_groups=mesh['sec'=4,'grp'=8] {'sec','grp'}, dimensions={0} | all-to-all | bytes 163840 | tf_op jit(solution)/shard_map/all_to_all | solution.py:554
  59.1 0.8 pixels.6
  60.0 9.1 %all_to_all.50 = f32[32,1,640]{2,1,0:T(1,128)S(1)} all-to-all(f32[32,1,640]{2,1,0:T(1,128)S(1)} %bitcast.33), channel_id=1, replica_groups=mesh['sec'=4,'grp'=8] {'sec','grp'}, dimensions={0} | all-to-all | bytes 163840 | tf_op jit(solution)/shard_map/all_to_all | solution.py:554
  69.1 0.0 copy-start.1
  69.1 1.1 %update.5 = (f32[160,128]{1,0:T(8,128)S(1)}, f32[4,8,1536]{2,1,0:T(8,128)S(1)}, f32[4,8,1536]{2,1,0:T(8,128)S(1)}) custom-call(f32[160,128]{1,0:T(8,128)S(1)} %bitcast.27, f32[1,128]{1,0:T(1,128)S(1)} %get-tuple-element.67.rr_ref.refs_2_, f32[2,1536]{1,0:T(2,128)S(1)} %copy-done, bf16[4,256,1536]{2,1,0:T(8,128)(2,1)S(1)} %get-tuple-element.48.refs_1_.legendre_ref, ...), custom_call_target="tpu_custom_call" | custom-call | tf_op jit(solution)/shard_map/update/pallas_call | solution.py:511
  70.2 9.1 %all_to_all.51 = f32[32,1,640]{2,1,0:T(1,128)S(1)} all-to-all(f32[32,1,640]{2,1,0:T(1,128)S(1)} %bitcast.35), channel_id=1, replica_groups=mesh['sec'=4,'grp'=8] {'sec','grp'}, dimensions={0} | all-to-all | bytes 163840 | tf_op jit(solution)/shard_map/all_to_all | solution.py:554
  79.3 0.8 pixels.7
  80.1 9.1 %all_to_all.52 = f32[32,1,640]{2,1,0:T(1,128)S(1)} all-to-all(f32[32,1,640]{2,1,0:T(1,128)S(1)} %bitcast.30), channel_id=1, replica_groups=mesh['sec'=4,'grp'=8] {'sec','grp'}, dimensions={0} | all-to-all | bytes 163840 | tf_op jit(solution)/shard_map/all_to_all | solution.py:554
  89.2 0.0 copy-done.1
  89.2 0.7 last.1
  89.9 8.8 %all_to_all.53 = f32[32,1,128]{2,1,0:T(1,128)S(1)} all-to-all(f32[32,1,128]{2,1,0:T(1,128)S(1)} %bitcast.39), channel_id=1, replica_groups=mesh['sec'=4,'grp'=8] {'sec','grp'}, dimensions={0} | all-to-all | bytes 32768 | tf_op jit(solution)/shard_map/all_to_all | solution.py:554
  98.7 0.8 end.1
Async XLA Ops:
  0.6 17.8 %copy-start = (f32[2,1536]{1,0:T(2,128)S(1)}, f32[2,1536]{1,0:T(2,128)}, u32[]{:S(2)}) copy-start(f32[2,1536]{1,0:T(2,128)} %prior_ref.15) | copy-start | bytes 36868
  0.6 17.8 %copy-start.5 = (s32[16,2048]{1,0:T(8,128)S(1)}, s32[16,2048]{1,0:T(8,128)}, u32[]{:S(2)}) copy-start(s32[16,2048]{1,0:T(8,128)} %refs_0_.1) | copy-start | bytes 393220
  0.7 17.8 %copy-start.4 = (f32[16,2048]{1,0:T(8,128)S(1)}, f32[16,2048]{1,0:T(8,128)}, u32[]{:S(2)}) copy-start(f32[16,2048]{1,0:T(8,128)} %uu_ref.1) | copy-start | bytes 393220
  0.7 17.8 %copy-start.3 = (f32[16,2048]{1,0:T(8,128)S(1)}, f32[16,2048]{1,0:T(8,128)}, u32[]{:S(2)}) copy-start(f32[16,2048]{1,0:T(8,128)} %qu_ref.1) | copy-start | bytes 393220
  0.7 17.8 %copy-start.2 = (f32[16,2048]{1,0:T(8,128)S(1)}, f32[16,2048]{1,0:T(8,128)}, u32[]{:S(2)}) copy-start(f32[16,2048]{1,0:T(8,128)} %qq_ref.1) | copy-start | bytes 393220
  69.1 20.1 %copy-start.1 = (f32[2,4,4,1536]{3,2,1,0:T(4,128)S(1)}, f32[2,4,4,1536]{3,2,1,0:T(4,128)}, u32[]{:S(2)}) copy-start(f32[2,4,4,1536]{3,2,1,0:T(4,128)} %solution_ref.1) | copy-start | bytes 589828
